TPU v7x, 32 devices: a whole 2x2x4 slice. The times are simulated.
32 devices in a mesh: tm: 8 (over y, x, core), stream: 4 (over z).
Axes of the slice: x: 2, y: 2, z: 4, core: 2. Of those that a mesh axis runs over, the one named last changes fastest.
Arguments:
- tokens: bfloat16 [4096, 2048], P(('tm', 'stream')), may hold values from -6 to 6
- w_query: bfloat16 [2048, 2048], P('stream'), may hold values from -0.125 to 0.125
- w_key: bfloat16 [2048, 2048], P('stream'), may hold values from -0.125 to 0.125
- w_value: bfloat16 [2048, 2048], P('stream'), may hold values from -0.125 to 0.125
- decay_proj: bfloat16 [2048, 16], P('stream'), may hold values from -0.125 to 0.125
- beta_proj: bfloat16 [2048, 16], P('stream'), may hold values from -0.125 to 0.125
- decay_rate: float32 [16], replicated, may hold values from 0.00024414062 to 0.1
- beta_bias: float32 [16], replicated, may hold values from -7 to 0
- norm_gain: float32 [128], replicated, may hold values from 0.5 to 1.5
Outputs:
- mixed: bfloat16 [4096, 2048], P(('tm', 'stream'))
All inputs are finite; a program needn't handle non-finite values.
Results may differ from a plain program's by a relative error of at most 0.0073.
Values may be sent and summed in bfloat16 or wider, within the bound.
A program may use at most 128 MiB of HBM per device.

v0:
```python
import functools

import jax
import jax.numpy as jnp
from jax import lax
from jax.experimental import pallas as pl
from jax.experimental.pallas import tpu as pltpu
from jax.sharding import PartitionSpec as P

HEADS = 16
DK = 128
DV = 128
CHUNK = 128
LANES = 128
F32 = jnp.float32
BF16 = jnp.bfloat16


def halves(a):
    high = a.astype(BF16)
    return high, (a - high.astype(F32)).astype(BF16)


def contract(a, b, dims):
    return lax.dot_general(a, b, dims, preferred_element_type=F32)


def dot3(a, b, ca, cb, batch=0):
    ah, al = halves(a)
    bh, bl = halves(b)
    free = batch + (cb - batch + 1) % 2
    lead = tuple(range(batch))
    wide = jnp.concatenate([bh, bl], free)
    both = contract(
        jnp.concatenate([ah, al], ca),
        jnp.concatenate([wide, wide], cb),
        (((ca,), (cb,)), (lead, lead)),
    )
    half = both.shape[-1] // 2
    return both[..., :half] + both[..., half:]


def around(count):
    return sorted(range(1, count), key=lambda i: min(i, count - i))


def gather_kernel(
    streams,
    places,
    heads,
    tok_ref,
    wq_ref,
    wk_ref,
    wv_ref,
    wg_ref,
    x_ref,
    full_ref,
    stage,
    load_sem,
    own_sem,
    tok_recv,
    right_sem,
    left_sem,
    cross_send,
    cross_recv,
    plane_send,
    pass_send,
    plane_recv,
):
    t = lax.axis_index("tm")
    z = lax.axis_index("stream")
    chips = places // 2
    chip = t // 2
    core = t % 2
    group = heads * DK

    loads = []
    for dest in range(streams):
        for j, ref in enumerate((wq_ref, wk_ref, wv_ref)):
            loads.append(
                pltpu.make_async_copy(
                    ref.at[t, :, pl.ds(dest * group, group)],
                    stage.at[dest, :, pl.ds(j * group, group)],
                    load_sem.at[dest, j],
                )
            )
        loads.append(
            pltpu.make_async_copy(
                wg_ref.at[t], stage.at[dest, :, pl.ds(3 * group, LANES)], load_sem.at[dest, 3]
            )
        )
    for copy in loads:
        copy.start()

    others = [(lax.rem(chip + i, chips) * 2 + core) for i in range(1, chips)]
    sibling = chip * 2 + 1 - core
    peers = [(t, lax.rem(z + i, streams)) for i in around(streams)]
    peers += [(sibling, z)] + [(o, z) for o in others]
    barrier = pltpu.get_barrier_semaphore()
    for peer in peers:
        pl.semaphore_signal(
            barrier, inc=1, device_id=peer, device_id_type=pl.DeviceIdType.MESH
        )
    pl.semaphore_wait(barrier, len(peers))
    for copy in loads:
        copy.wait()

    def remote(src, dst, send, recv, device):
        return pltpu.make_async_remote_copy(
            src_ref=src,
            dst_ref=dst,
            send_sem=send,
            recv_sem=recv,
            device_id=device,
            device_id_type=pl.DeviceIdType.MESH,
        )

    def cross(i):
        dest = lax.rem(z + i, streams)
        return remote(
            stage.at[dest], full_ref.at[t, z], cross_send.at[dest], cross_recv.at[z], (t, dest)
        )

    def crossed(i):
        s = lax.rem(z + i, streams)
        return remote(
            stage.at[s], full_ref.at[t, s], cross_send.at[s], cross_recv.at[s], (t, s)
        )

    def line(chunk, right, first):
        src = tok_ref if first else x_ref.at[chunk]
        send = (right_sem if right else left_sem).at[chunk]
        return remote(
            src, x_ref.at[chunk], send, tok_recv.at[chunk], (t, z + 1 if right else z - 1)
        )

    def plane(i, s, first):
        to = sibling if i == 0 else others[i - 1]
        src = stage.at[z] if first else full_ref.at[t, s]
        return remote(
            src, full_ref.at[t, s], plane_send.at[i, s], plane_recv.at[t, s], (to, z)
        )

    def relay(i, s):
        at = others[i - 1]
        here = full_ref.at[at, s]
        return remote(here, here, pass_send.at[i, s], plane_recv.at[at, s], (sibling, z))

    def landed(at, s):
        here = full_ref.at[at, s]
        return remote(here, here, plane_send.at[0, s], plane_recv.at[at, s], (sibling, z))

    for i in around(streams):
        cross(i).start()

    @pl.when(z < streams - 1)
    def _():
        line(z, True, True).start()

    @pl.when(z > 0)
    def _():
        line(z, False, True).start()

    for i in range(1, chips):
        plane(i, z, True).start()
    plane(0, z, True).start()
    own = [
        pltpu.make_async_copy(stage.at[z], full_ref.at[t, z], own_sem.at[0]),
        pltpu.make_async_copy(tok_ref, x_ref.at[z], own_sem.at[1]),
    ]
    for copy in own:
        copy.start()

    for i in around(streams):
        s = lax.rem(z + i, streams)
        crossed(i).wait_recv()
        for j in range(1, chips):
            plane(j, s, False).start()
        plane(0, s, False).start()

    def step(k):
        @pl.when(z >= k)
        def _():
            line(z - k, True, False).wait_recv()

            @pl.when(z < streams - 1)
            def _():
                line(z - k, True, False).start()

        @pl.when(z + k < streams)
        def _():
            line(z + k, False, False).wait_recv()

            @pl.when(z > 0)
            def _():
                line(z + k, False, False).start()

    orders = [z] + [lax.rem(z + i, streams) for i in around(streams)]
    passed = 0
    for k in range(1, streams):
        step(k)
        upto = len(orders) if k == streams - 2 else passed + 1
        while passed < min(upto, len(orders)):
            s = orders[passed]
            for i in range(1, chips):
                landed(others[i - 1], s).wait_recv()
                relay(i, s).start()
            passed += 1
    while passed < len(orders):
        s = orders[passed]
        for i in range(1, chips):
            landed(others[i - 1], s).wait_recv()
            relay(i, s).start()
        passed += 1

    for copy in own:
        copy.wait()
    for s in orders:
        landed(sibling, s).wait_recv()
        for i in range(1, chips):
            landed(lax.rem(chip + i, chips) * 2 + 1 - core, s).wait_recv()
    for i in around(streams):
        cross(i).wait_send()
    for n, s in enumerate(orders):
        for i in range(chips):
            plane(i, s, n == 0).wait_send()
        for i in range(1, chips):
            relay(i, s).wait_send()
    for k in range(streams):

        @pl.when((z >= k) & (z < streams - 1))
        def _():
            line(z - k, True, k == 0).wait_send()

        @pl.when((z + k < streams) & (z > 0))
        def _():
            line(z + k, False, k == 0).wait_send()


def block_kernel(
    heads,
    x_ref,
    w_ref,
    rate_ref,
    bias_ref,
    read_ref,
    query_ref,
    state_ref,
    cum,
    cum_row,
    beta,
):
    first_head = lax.axis_index("stream") * heads
    rows = x_ref.shape[0]
    places, streams, share, _ = w_ref.shape
    depth = places * share

    def project(groups):
        total = None
        for s in range(streams):
            parts = [w_ref[:, s, :, pl.ds(pl.multiple_of(at * LANES, LANES), LANES)] for at in groups]
            w = jnp.concatenate([part.reshape(depth, LANES) for part in parts], 1)
            term = contract(x_ref[:, s * depth : (s + 1) * depth], w, (((1,), (0,)), ((), ())))
            total = term if total is None else total + term
        return total

    chunks = rows // CHUNK
    row_at = lax.broadcasted_iota(jnp.int32, (CHUNK, CHUNK), 0)
    col_at = lax.broadcasted_iota(jnp.int32, (CHUNK, CHUNK), 1)

    logits = project((3 * heads,))
    soft = jnp.maximum(logits, 0.0) + jnp.log1p(jnp.exp(-jnp.abs(logits)))
    decay = (-rate_ref[...] * soft).astype(BF16)
    beta[...] = (
        (1.0 / (1.0 + jnp.exp(-(logits + bias_ref[...])))).astype(BF16).astype(F32)
    ).reshape(chunks, CHUNK, LANES)
    lower_ones = jnp.where(row_at >= col_at, 1.0, 0.0).astype(BF16)
    for c in range(chunks):
        piece = decay[c * CHUNK : (c + 1) * CHUNK]
        sums = contract(lower_ones, piece, (((1,), (0,)), ((), ())))
        cum[c] = sums
        cum_row[c] = sums.T

    qs, ks, vs, gs, bs, g_rows = [], [], [], [], [], []
    lane = lax.broadcasted_iota(jnp.int32, (chunks, CHUNK, LANES), 2)
    for h in range(heads):
        raw = project([h + j * heads for j in range(3)])
        raw_q = raw[:, :DK]
        raw_k = raw[:, DK : 2 * DK]
        q = (
            raw_q * lax.rsqrt(jnp.sum(raw_q * raw_q, -1, keepdims=True) + 1e-06) * DK ** (-0.5)
        ).astype(BF16)
        k = (raw_k * lax.rsqrt(jnp.sum(raw_k * raw_k, -1, keepdims=True) + 1e-06)).astype(BF16)
        v = raw[:, 2 * DK :].astype(BF16)
        qs.append(q.reshape(chunks, CHUNK, DK))
        ks.append(k.reshape(chunks, CHUNK, DK))
        vs.append(v.reshape(chunks, CHUNK, DV))
        head = first_head + h
        gs.append(jnp.sum(jnp.where(lane == head, cum[...], 0.0), -1, keepdims=True))
        bs.append(jnp.sum(jnp.where(lane == head + HEADS, beta[...], 0.0), -1, keepdims=True))
        g_rows.append(cum_row[:, pl.ds(head, 1), :])
    q, k, v, g, b, g_row = (jnp.concatenate(a, 0) for a in (qs, ks, vs, gs, bs, g_rows))
    v = v.astype(F32)
    g_last = g[:, CHUNK - 1 :, :]
    growth = jnp.exp(g)
    tail = jnp.exp(g_last - g)
    whole = jnp.exp(g_last)

    batched = (((2,), (2,)), ((0,), (0,)))
    pair = contract(jnp.concatenate([k, q], 1), k, batched)
    low = row_at >= col_at
    spread = jnp.exp(jnp.where(low[None], g - g_row, 0.0))
    lmat = jnp.where((row_at > col_at)[None], b * spread * pair[:, :CHUNK], 0.0)
    mmat = jnp.where(low[None], spread * pair[:, CHUNK:], 0.0)

    eye = jnp.where(row_at == col_at, 1.0, 0.0)
    inverse = None
    size = 1
    while size < CHUNK:
        inside = (row_at // (2 * size) == col_at // (2 * size)) & (row_at // size != col_at // size)
        off = jnp.where(inside[None], lmat, 0.0)
        if inverse is None:
            inverse = eye[None] - off
        else:
            inverse = inverse - dot3(inverse, dot3(off, inverse, 2, 1, 1), 2, 1, 1)
        size *= 2

    kf = k.astype(F32)
    right = jnp.concatenate([(b * growth) * kf, b * v], 2)
    wu = dot3(inverse, right, 2, 1, 1)
    mwu = dot3(mmat, wu, 2, 1, 1)
    moved = growth * q.astype(F32) - mwu[:, :, :DK]
    key_tail = tail * kf
    jumps = dot3(jnp.swapaxes(wu, 1, 2), key_tail, 2, 1, 1)
    step_map = whole * eye[None] - jumps[:, :DK]

    carries = [None] * heads
    for c in range(chunks):
        at = slice(c * CHUNK, (c + 1) * CHUNK)
        for h in range(heads):
            n = h * chunks + c
            lanes = slice(h * DK, (h + 1) * DK)
            if c == 0:
                query_ref[at, lanes] = moved[n]
                read_ref[at, lanes] = mwu[n, :, DK:]
                carries[h] = jnp.concatenate([step_map[n], jumps[n, DK:]], 0)
                continue
            both = dot3(moved[n], carries[h], 1, 1)
            query_ref[at, lanes] = both[:, :DK]
            read_ref[at, lanes] = mwu[n, :, DK:] + both[:, DK:]
            carry = dot3(carries[h], step_map[n], 1, 0)
            carries[h] = jnp.concatenate([carry[:DK], carry[DK:] + jumps[n, DK:]], 0)
    for h in range(heads):
        state_ref[h] = carries[h]


def return_kernel(
    streams,
    places,
    heads,
    read_ref,
    query_ref,
    maps_ref,
    gain_ref,
    out_ref,
    pair,
    total,
    got,
    carried,
    state,
    mixed,
    pair_sem,
    state_sem,
    chip_send,
    chip_recv,
    out_send,
    out_recv,
    own_sem,
):
    t = lax.axis_index("tm")
    z = lax.axis_index("stream")
    chips = places // 2
    chip = t // 2
    core = t % 2
    sibling = chip * 2 + 1 - core
    group = heads * DV
    local = out_ref.shape[0]

    peers = [(t, lax.rem(z + i, streams)) for i in around(streams)]
    peers += [(sibling, z)]
    peers += [(lax.rem(chip + i, chips) * 2 + core, z) for i in range(1, chips)]
    barrier = pltpu.get_barrier_semaphore()
    for peer in peers:
        pl.semaphore_signal(
            barrier, inc=1, device_id=peer, device_id_type=pl.DeviceIdType.MESH
        )
    pl.semaphore_wait(barrier, len(peers))

    def remote(src, dst, send, recv, device):
        return pltpu.make_async_remote_copy(
            src_ref=src,
            dst_ref=dst,
            send_sem=send,
            recv_sem=recv,
            device_id=device,
            device_id_type=pl.DeviceIdType.MESH,
        )

    def hand_over():
        return remote(maps_ref, pair, pair_sem.at[0], pair_sem.at[1], (sibling, z))

    def hand_back():
        return remote(carried, carried, state_sem.at[0], state_sem.at[1], (sibling, z))

    def to_chip(source, dest):
        src, dst = total, got.at[source]
        if source == 0:
            src, dst = total.at[:, pl.ds(DK, DV)], got.at[0, :, pl.ds(DK, DV)]
        return remote(src, dst, chip_send.at[dest], chip_recv.at[source], (dest * 2 + 1, z))

    @pl.when(core == 0)
    def _():
        hand_over().start()
        hand_over().wait_send()

    @pl.when(core == 1)
    def _():
        hand_over().wait_recv()

        @pl.when(chip < chips - 1)
        def _():
            for h in range(heads):
                both = dot3(pair[h], maps_ref[h, :DK], 1, 0)
                total[h, :DK] = both[:DK]
                total[h, DK:] = both[DK:] + maps_ref[h, DK:]

        for source in range(chips - 1):

            @pl.when(chip == source)
            def _():
                for dest in range(chips - 1, source, -1):
                    to_chip(source, dest).start()

        for source in range(chips - 1):

            @pl.when(chip > source)
            def _():
                to_chip(source, chip).wait_recv()
                for h in range(heads):
                    if source == 0:
                        carried[h] = got[0, h, DK:]
                    else:
                        carried[h] = dot3(carried[h], got[source, h, :DK], 1, 0) + got[source, h, DK:]

        @pl.when(chip > 0)
        def _():
            hand_back().start()
            for h in range(heads):
                state[h] = dot3(carried[h], pair[h, :DK], 1, 0) + pair[h, DK:]

        @pl.when(chip == 0)
        def _():
            for h in range(heads):
                state[h] = pair[h, DK:]

    @pl.when((core == 0) & (chip > 0))
    def _():
        hand_back().wait_recv()
        for h in range(heads):
            state[h] = carried[h]

    @pl.when((core == 0) & (chip == 0))
    def _():
        state[...] = jnp.zeros_like(state)

    def outgoing(i):
        dest = lax.rem(z + i, streams)
        dst = out_ref.at[:, pl.ds(pl.multiple_of(z * group, group), group)]
        return remote(mixed.at[dest], dst, out_send.at[dest], out_recv.at[z], (t, dest))

    def incoming(i):
        source = lax.rem(z + i, streams)
        dst = out_ref.at[:, pl.ds(pl.multiple_of(source * group, group), group)]
        return remote(mixed.at[source], dst, out_send.at[source], out_recv.at[source], (t, source))

    own = pltpu.make_async_copy(
        mixed.at[z], out_ref.at[:, pl.ds(pl.multiple_of(z * group, group), group)], own_sem.at[0]
    )
    order = list(reversed(around(streams)))
    for i in order + [0]:
        dest = lax.rem(z + i, streams)
        at = pl.ds(pl.multiple_of(dest * local, local), local)
        for h in range(heads):
            lanes = slice(h * DV, (h + 1) * DV)
            read = read_ref[at, lanes] + dot3(query_ref[at, lanes], state[h], 1, 1)
            readout = read.astype(BF16).astype(F32)
            scale = lax.rsqrt(jnp.mean(readout * readout, -1, keepdims=True) + 1e-06)
            mixed[dest, :, lanes] = (readout * scale * gain_ref[...]).astype(BF16)
        if i == 0:
            own.start()
        else:
            outgoing(i).start()

    own.wait()
    for i in order:
        incoming(i).wait_recv()
    for i in order:
        outgoing(i).wait_send()

    @pl.when((core == 1) & (chip > 0))
    def _():
        hand_back().wait_send()

    for source in range(chips - 1):

        @pl.when((core == 1) & (chip == source))
        def _():
            for dest in range(chips - 1, source, -1):
                to_chip(source, dest).wait_send()


def shards(
    tokens, w_query, w_key, w_value, decay_proj, beta_proj, decay_rate, beta_bias, norm_gain
):
    streams = lax.axis_size("stream")
    places = lax.axis_size("tm")
    heads = HEADS // streams
    depth = w_query.shape[0]
    share = depth // places
    width = 3 * heads * DK + LANES
    gates = jnp.pad(
        jnp.concatenate([decay_proj, beta_proj], 1), ((0, 0), (0, LANES - 2 * HEADS))
    )
    shares = [w.reshape(places, share, -1) for w in (w_query, w_key, w_value, gates)]
    local, features = tokens.shape
    any_space = pl.BlockSpec(memory_space=pl.ANY)
    dma = pltpu.SemaphoreType.DMA
    chips = places // 2
    x, full = pl.pallas_call(
        functools.partial(gather_kernel, streams, places, heads),
        out_shape=(
            jax.ShapeDtypeStruct((streams, local, features), BF16),
            jax.ShapeDtypeStruct((places, streams, share, width), BF16),
        ),
        in_specs=[pl.BlockSpec(memory_space=pltpu.VMEM)] + [any_space] * 4,
        out_specs=(any_space, any_space),
        scratch_shapes=[
            pltpu.VMEM((streams, share, width), BF16),
            dma((streams, 4)),
            dma((2,)),
            dma((streams,)),
            dma((streams,)),
            dma((streams,)),
            dma((streams,)),
            dma((streams,)),
            dma((chips, streams)),
            dma((chips, streams)),
            dma((places, streams)),
        ],
        compiler_params=pltpu.CompilerParams(collective_id=0, has_side_effects=True),
    )(tokens, *shares)
    x = x.reshape(streams * local, features)
    rows = x.shape[0]
    if share % 16:
        full = full.transpose(1, 0, 2, 3).reshape(1, streams, places * share, width)

    rate = jnp.pad(decay_rate, (0, LANES - HEADS))[None]
    bias = jnp.pad(beta_bias, (HEADS, LANES - 2 * HEADS))[None]

    chunks = rows // CHUNK
    read, moved, maps = pl.pallas_call(
        functools.partial(block_kernel, heads),
        out_shape=(
            jax.ShapeDtypeStruct((rows, heads * DV), F32),
            jax.ShapeDtypeStruct((rows, heads * DK), F32),
            jax.ShapeDtypeStruct((heads, DK + DV, DK), F32),
        ),
        in_specs=[pl.BlockSpec(memory_space=pltpu.VMEM)] * 4,
        out_specs=(pl.BlockSpec(memory_space=pltpu.VMEM),) * 3,
        scratch_shapes=[
            pltpu.VMEM((chunks, CHUNK, LANES), F32),
            pltpu.VMEM((chunks, LANES, CHUNK), F32),
            pltpu.VMEM((chunks, CHUNK, LANES), F32),
        ],
    )(x, full, rate, bias)

    vmem = pl.BlockSpec(memory_space=pltpu.VMEM)
    return pl.pallas_call(
        functools.partial(return_kernel, streams, places, heads),
        out_shape=jax.ShapeDtypeStruct((local, HEADS * DV), BF16),
        in_specs=[vmem] * 4,
        out_specs=any_space,
        scratch_shapes=[
            pltpu.VMEM((heads, DK + DV, DK), F32),
            pltpu.VMEM((heads, DK + DV, DK), F32),
            pltpu.VMEM((chips, heads, DK + DV, DK), F32),
            pltpu.VMEM((heads, DV, DK), F32),
            pltpu.VMEM((heads, DV, DK), F32),
            pltpu.VMEM((streams, local, heads * DV), BF16),
            dma((2,)),
            dma((2,)),
            dma((chips,)),
            dma((chips,)),
            dma((streams,)),
            dma((streams,)),
            dma((1,)),
        ],
        compiler_params=pltpu.CompilerParams(collective_id=1, has_side_effects=True),
    )(read, moved, maps, norm_gain[None])


def solution(mesh):
    return jax.shard_map(
        shards,
        mesh=mesh,
        in_specs=(
            P(("tm", "stream"), None),
            P("stream", None),
            P("stream", None),
            P("stream", None),
            P("stream", None),
            P("stream", None),
            P(),
            P(),
            P(),
        ),
        out_specs=P(("tm", "stream"), None),
        check_vma=False,
    )
```

profile of v0, /device:TPU:4, one launch (start us, length us, event | category | flops | bytes accessed | tf_op | source)
XLA Modules:
  0.0 112.2 jit_solution(6841140299947538880)
XLA Ops:
  0.0 1.3 %pad_bitcast_fusion = (f32[1,128]{1,0:T(1,128)}, f32[1,128]{1,0:T(1,128)}) fusion(f32[16]{0:T(128)} %param.16, f32[16]{0:T(128)} %param.15), kind=kLoop, calls=%fused_computation.1 | loop fusion | bytes 1152 | tf_op jit(solution)/shard_map/broadcast_in_dim | solution.py:568
  1.3 0.7 pad_maximum_fusion
  2.0 0.1 copy.11
  2.2 0.7 pad.12.clone
  2.8 59.5 %shard_map.91 = (bf16[4,128,2048]{2,1,0:T(8,128)(2,1)}, bf16[8,4,64,1664]{3,2,1,0:T(8,128)(2,1)}) custom-call(bf16[128,2048]{1,0:T(8,128)(2,1)} %tok_ref.1, bf16[8,64,2048]{2,1,0:T(8,128)(2,1)} %bitcast.11, bf16[8,64,2048]{2,1,0:T(8,128)(2,1)} %bitcast.12, bf16[8,64,2048]{2,1,0:T(8,128)(2,1)} %bitcast.13, bf16[8,64,128]{2,1,0:T(8,128)(2,1)} %bitcast.14), custom_call_target="tpu_custom_call" | custom-call | tf_op jit(solution)/shard_map/pallas_call | solution.py:539
  62.4 19.0 %shard_map.92 = (f32[512,512]{1,0:T(8,128)}, f32[512,512]{1,0:T(8,128)}, f32[4,256,128]{2,1,0:T(8,128)}) custom-call(bf16[512,2048]{1,0:T(8,128)(2,1)} %bitcast.10, bf16[8,4,64,1664]{3,2,1,0:T(8,128)(2,1)} %get-tuple-element.11.w_ref, f32[1,128]{1,0:T(1,128)} %get-tuple-element.16.rate_ref, f32[1,128]{1,0:T(1,128)} %get-tuple-element.15.bias_ref), custom_call_target="tpu_custom_call" | custom-call | tf_op jit(solution)/shard_map/pallas_call | solution.py:571
  81.4 28.9 %shard_map.93 = bf16[128,2048]{1,0:T(8,128)(2,1)} custom-call(f32[512,512]{1,0:T(8,128)} %get-tuple-element.12.read_ref, f32[512,512]{1,0:T(8,128)} %get-tuple-element.13.query_ref, f32[4,256,128]{2,1,0:T(8,128)} %get-tuple-element.14.maps_ref, f32[1,128]{1,0:T(1,128)} %bitcast.15), custom_call_target="tpu_custom_call" | custom-call | tf_op jit(solution)/shard_map/pallas_call | solution.py:588
  110.3 1.9 %copy.13 = bf16[128,2048]{1,0:T(8,128)(2,1)} copy(bf16[128,2048]{1,0:T(8,128)(2,1)} %shard_map.93) | data formatting | bytes 1048576
where the time goes:
time: 113 us; the launch traced here: 112 us
  Pallas kernels  107 us (95%)
  local copies, waits for them, and re-layouts  3.98 us (4%)
    pallas_call x1, Pallas kernels, shards(): pl.pallas_call(functools.partial(gather_kernel, streams, places, heads),...  59.5 us
    pallas_call x1, Pallas kernels, shards(): pl.pallas_call(functools.partial(return_kernel, streams, places, heads),...  28.9 us
    pallas_call x1, Pallas kernels, shards(): pl.pallas_call(functools.partial(block_kernel, heads), out_shape=(jax.Sha...  19 us

commit v1 on v0

v1 whole, which is shorter than its diff:
```python
import functools

import jax
import jax.numpy as jnp
from jax import lax
from jax.experimental import pallas as pl
from jax.experimental.pallas import tpu as pltpu
from jax.sharding import PartitionSpec as P

HEADS = 16
DK = 128
DV = 128
CHUNK = 128
WIDTH = 2 * DK + DV
PIECES = 4
EARLY = 2
F32 = jnp.float32
BF16 = jnp.bfloat16


def halves(a):
    high = a.astype(BF16)
    return high, (a - high.astype(F32)).astype(BF16)


def contract(a, b, dims):
    return lax.dot_general(a, b, dims, preferred_element_type=F32)


def dot3(a, b, ca, cb, batch=0):
    ah, al = halves(a)
    bh, bl = halves(b)
    free = batch + (cb - batch + 1) % 2
    lead = tuple(range(batch))
    wide = jnp.concatenate([bh, bl], free)
    both = contract(
        jnp.concatenate([ah, al], ca),
        jnp.concatenate([wide, wide], cb),
        (((ca,), (cb,)), (lead, lead)),
    )
    half = both.shape[-1] // 2
    return both[..., :half] + both[..., half:]


def dot2(a, b, ca, cb):
    ah, al = halves(a)
    return contract(
        jnp.concatenate([ah, al], ca), jnp.concatenate([b, b], cb), (((ca,), (cb,)), ((), ()))
    )


def around(count):
    return sorted(range(1, count), key=lambda i: min(i, count - i))


def layer_kernel(
    streams,
    places,
    heads,
    senders,
    tok_ref,
    wq_ref,
    wk_ref,
    wv_ref,
    dec_ref,
    bet_ref,
    rate_ref,
    bias_ref,
    gain_ref,
    out_ref,
    x_ref,
    full,
    stage,
    gates,
    cum,
    cum_row,
    beta,
    read_ref,
    query_ref,
    own_map,
    sent_map,
    sib_map,
    total,
    got,
    prev,
    mixed,
    load_sem,
    own_sem,
    gate_load,
    tok_load,
    gate_send,
    gate_recv,
    gate_pass,
    gate_sib,
    right_sem,
    left_sem,
    tok_recv,
    cross_send,
    cross_recv,
    plane_send,
    pass_send,
    plane_recv,
    pair_send,
    pair_recv,
    chip_send,
    chip_recv,
    out_send,
    out_recv,
    out_own,
):
    t = lax.axis_index("tm")
    z = lax.axis_index("stream")
    chips = places // 2
    chip = t // 2
    core = t % 2
    sibling = chip * 2 + 1 - core
    depth = wq_ref.shape[0]
    share = depth // senders
    stride = places // senders
    step = max(stride // 2, 1)
    paired = stride == 1
    origins = senders // 2 if paired else senders
    base = chip // step * step
    local = tok_ref.shape[0]
    part = local // PIECES
    rows = streams * local
    chunks = rows // CHUNK
    near = around(streams)

    def remote(src, dst, send, recv, device):
        return pltpu.make_async_remote_copy(
            src_ref=src,
            dst_ref=dst,
            send_sem=send,
            recv_sem=recv,
            device_id=device,
            device_id_type=pl.DeviceIdType.MESH,
        )

    def only(cond, body):
        if cond is True:
            body()
        elif cond is not False:
            pl.when(cond)(body)

    is_sender = True if paired else (t % stride == 0)
    active = True if paired else (core == 0)
    mine = t // stride

    def slot(i):
        at = lax.rem(base + i * step, chips)
        return at, (2 * at + core if paired else at // step)

    weights = (wq_ref, wk_ref, wv_ref)

    own_gates = [
        pltpu.make_async_copy(dec_ref, gates.at[0, z], gate_load.at[0]),
        pltpu.make_async_copy(bet_ref, gates.at[1, z], gate_load.at[1]),
    ]
    for copy in own_gates:
        copy.start()

    def load_stage():
        for h in range(heads):
            for i in near:
                dest = lax.rem(z + i, streams)
                for j, ref in enumerate(weights):
                    cols = pl.ds(pl.multiple_of((dest * heads + h) * DK, DK), DK)
                    at = pl.ds(pl.multiple_of(mine * share, share), share)
                    pltpu.make_async_copy(
                        ref.at[at, cols],
                        stage.at[dest, h, :, pl.ds(j * DK, DK)],
                        load_sem.at[dest, h],
                    ).start()

    only(is_sender, load_stage)
    own_tok = pltpu.make_async_copy(tok_ref, x_ref.at[z], tok_load.at[0])
    own_tok.start()
    for h in range(heads):
        for j, ref in enumerate(weights):
            cols = pl.ds(pl.multiple_of((z * heads + h) * DK, DK), DK)
            pltpu.make_async_copy(
                ref.at[:, cols], full.at[h, z, :, pl.ds(j * DK, DK)], own_sem.at[h]
            ).start()

    others = [lax.rem(chip + i, chips) * 2 + core for i in range(1, chips)]
    peers = [(t, lax.rem(z + i, streams)) for i in near]
    peers += [(sibling, z)] + [(o, z) for o in others]
    barrier = pltpu.get_barrier_semaphore()
    for peer in peers:
        pl.semaphore_signal(
            barrier, inc=1, device_id=peer, device_id_type=pl.DeviceIdType.MESH
        )
    pl.semaphore_wait(barrier, len(peers))

    def line(s, p, right, first):
        at = pl.ds(p * part, part)
        src = tok_ref.at[at] if first else x_ref.at[s, at]
        send = (right_sem if right else left_sem).at[s, p]
        return remote(
            src, x_ref.at[s, at], send, tok_recv.at[s, p], (t, z + 1 if right else z - 1)
        )

    def gate_out(i):
        dest = lax.rem(z + i, streams)
        here = gates.at[core, z]
        return remote(here, here, gate_send.at[dest], gate_recv.at[z], (t, dest))

    def gate_in(i):
        s = lax.rem(z + i, streams)
        here = gates.at[core, s]
        return remote(here, here, gate_send.at[s], gate_recv.at[s], (t, s))

    def gate_on(i):
        s = lax.rem(z + i, streams)
        here = gates.at[core, s]
        return remote(here, here, gate_pass.at[s], gate_sib.at[s], (sibling, z))

    def gate_landed(i):
        s = lax.rem(z + i, streams)
        here = gates.at[1 - core, s]
        return remote(here, here, gate_pass.at[s], gate_sib.at[s], (sibling, z))

    def rows_of(k):
        return pl.ds(pl.multiple_of(k * share, share), share)

    def cross(u, i):
        dest = lax.rem(z + i, streams)
        return remote(
            stage.at[dest, u],
            full.at[u, z, rows_of(mine)],
            cross_send.at[dest, u],
            cross_recv.at[z, u],
            (t, dest),
        )

    def crossed(u, i):
        s = lax.rem(z + i, streams)
        return remote(
            stage.at[s, u],
            full.at[u, s, rows_of(mine)],
            cross_send.at[s, u],
            cross_recv.at[s, u],
            (t, s),
        )

    def plane(u, i, s):
        to = sibling if i == 0 else others[i - 1]
        here = full.at[u, s, rows_of(mine)]
        return remote(
            here, here, plane_send.at[i, s, u], plane_recv.at[mine, s, u], (to, z)
        )

    def relay(u, i, s):
        k = slot(i)[1]
        here = full.at[u, s, rows_of(k)]
        return remote(here, here, pass_send.at[i, s, u], plane_recv.at[k, s, u], (sibling, z))

    def landed(u, k, s):
        here = full.at[u, s, rows_of(k)]
        return remote(here, here, plane_send.at[0, s, u], plane_recv.at[k, s, u], (sibling, z))

    def issue(u):
        def body():
            for i in near:
                dest = lax.rem(z + i, streams)
                pltpu.make_async_copy(
                    stage.at[dest, u], stage.at[dest, u], load_sem.at[dest, u]
                ).wait()
                cross(u, i).start()

        only(is_sender, body)

    def spread(u):
        def body():
            for i in near:
                s = lax.rem(z + i, streams)
                crossed(u, i).wait_recv()
                for j in range(1, chips):
                    plane(u, j, s).start()
                plane(u, 0, s).start()

        only(is_sender, body)

    def pass_on(u):
        for i in range(origins):
            at, k = slot(i)
            if i == 0:
                if paired:
                    continue
                cond = active & (chip != base)
            else:
                cond = active

            def body(i=i, k=k):
                for n in near:
                    s = lax.rem(z + n, streams)
                    landed(u, k, s).wait_recv()
                    relay(u, i, s).start()

            only(cond, body)

    def arrived(u):
        def body():
            for k in range(origins):
                origin = 2 * k + 1 - core if paired else k
                for n in near:
                    landed(u, origin, lax.rem(z + n, streams)).wait_recv()

        only(True if paired else core == 1, body)
        pltpu.make_async_copy(full.at[u, z], full.at[u, z], own_sem.at[u]).wait()

    def token_step(k, p):
        @pl.when(z >= k)
        def _():
            line(z - k, p, True, False).wait_recv()

            @pl.when(z < streams - 1)
            def _():
                line(z - k, p, True, False).start()

        @pl.when(z + k < streams)
        def _():
            line(z + k, p, False, False).wait_recv()

            @pl.when(z > 0)
            def _():
                line(z + k, p, False, False).start()

    for copy in own_gates:
        copy.wait()
    for i in near:
        gate_out(i).start()
    for p in range(PIECES):

        @pl.when(z < streams - 1)
        def _():
            line(z, p, True, True).start()

        @pl.when(z > 0)
        def _():
            line(z, p, False, True).start()

    early = range(min(EARLY, heads))
    late = range(min(EARLY, heads), heads)
    for u in early:
        issue(u)
    for k in range(1, streams):
        for p in range(PIECES):
            token_step(k, p)
        if k == 1:
            for i in near:
                gate_in(i).wait_recv()
                gate_on(i).start()
            for u in early:
                spread(u)
        if k == max(streams - 2, 1):
            for u in late:
                issue(u)
            for u in early:
                pass_on(u)
    own_tok.wait()
    for i in near:
        gate_landed(i).wait_recv()

    row_at = lax.broadcasted_iota(jnp.int32, (CHUNK, CHUNK), 0)
    col_at = lax.broadcasted_iota(jnp.int32, (CHUNK, CHUNK), 1)
    low = row_at >= col_at
    strict = row_at > col_at
    eye = jnp.where(row_at == col_at, 1.0, 0.0)
    lower_ones = jnp.where(low, 1.0, 0.0).astype(BF16)

    def logits(which):
        sums = None
        for s in range(streams):
            x = x_ref[:, :, pl.ds(s * depth, depth)].reshape(rows, depth)
            term = contract(x, gates[which, s], (((1,), (1,)), ((), ())))
            sums = term if sums is None else sums + term
        return sums

    first = logits(0)
    soft = jnp.maximum(first, 0.0) + jnp.log1p(jnp.exp(-jnp.abs(first)))
    decay = (-rate_ref[...] * soft).astype(BF16)
    beta[...] = (
        (1.0 / (1.0 + jnp.exp(-(logits(1) + bias_ref[...])))).astype(BF16).astype(F32)
    ).reshape(chunks, CHUNK, HEADS)
    for c in range(chunks):
        sums = contract(
            lower_ones, decay[c * CHUNK : (c + 1) * CHUNK], (((1,), (0,)), ((), ()))
        )
        cum[c] = sums
        cum_row[c] = sums.T

    lane = lax.broadcasted_iota(jnp.int32, (chunks, CHUNK, HEADS), 2)

    def pair_copy(h):
        return remote(
            sent_map.at[h], sib_map.at[h], pair_send.at[h], pair_recv.at[h], (sibling, z)
        )

    def to_chip(h, source, dest):
        src, dst = total.at[h], got.at[source, h]
        if source == 0:
            src, dst = total.at[h, pl.ds(DK, DV)], got.at[0, h, pl.ds(DK, DV)]
        return remote(
            src, dst, chip_send.at[dest, h], chip_recv.at[source, h], (dest * 2 + core, z)
        )

    def compute(h):
        x = x_ref[...].reshape(rows, x_ref.shape[2])
        w = full[h].reshape(streams * depth, WIDTH)
        raw = contract(x, w, (((1,), (0,)), ((), ())))
        raw_q = raw[:, :DK]
        raw_k = raw[:, DK : 2 * DK]
        q = (
            raw_q * lax.rsqrt(jnp.sum(raw_q * raw_q, -1, keepdims=True) + 1e-06) * DK ** (-0.5)
        ).astype(BF16)
        k = (raw_k * lax.rsqrt(jnp.sum(raw_k * raw_k, -1, keepdims=True) + 1e-06)).astype(BF16)
        v = raw[:, 2 * DK :].astype(BF16)
        q = q.reshape(chunks, CHUNK, DK)
        k = k.reshape(chunks, CHUNK, DK)
        v = v.reshape(chunks, CHUNK, DV).astype(F32)
        head = z * heads + h
        g = jnp.sum(jnp.where(lane == head, cum[...], 0.0), -1, keepdims=True)
        b = jnp.sum(jnp.where(lane == head, beta[...], 0.0), -1, keepdims=True)
        g_row = cum_row[:, pl.ds(head, 1), :]
        g_last = g[:, CHUNK - 1 :, :]
        growth = jnp.exp(g)
        tail = jnp.exp(g_last - g)
        whole = jnp.exp(g_last)

        pair = contract(jnp.concatenate([k, q], 1), k, (((2,), (2,)), ((0,), (0,))))
        spread_ = jnp.exp(jnp.where(low[None], g - g_row, 0.0))
        lmat = jnp.where(strict[None], b * spread_ * pair[:, :CHUNK], 0.0)
        mmat = jnp.where(low[None], spread_ * pair[:, CHUNK:], 0.0)

        inverse = None
        size = 1
        while size < CHUNK:
            inside = (row_at // (2 * size) == col_at // (2 * size)) & (
                row_at // size != col_at // size
            )
            off = jnp.where(inside[None], lmat, 0.0)
            if inverse is None:
                inverse = eye[None] - off
            else:
                inverse = inverse - dot3(inverse, dot3(off, inverse, 2, 1, 1), 2, 1, 1)
            size *= 2

        kf = k.astype(F32)
        right = jnp.concatenate([(b * growth) * kf, b * v], 2)
        wu = dot3(inverse, right, 2, 1, 1)
        key_tail = tail * kf
        jumps = dot3(jnp.swapaxes(wu, 1, 2), key_tail, 2, 1, 1)
        step_map = whole * eye[None] - jumps[:, :DK]
        carry = jnp.concatenate([step_map[0], jumps[0, DK:]], 0)
        carries = [carry]
        for c in range(1, chunks):
            moved = dot3(carry, step_map[c], 1, 0)
            carry = jnp.concatenate([moved[:DK], moved[DK:] + jumps[c, DK:]], 0)
            carries.append(carry)
        own_map[h] = carry
        sent_map[h] = carry.astype(BF16)
        pair_copy(h).start()

        mwu = dot3(mmat, wu, 2, 1, 1)
        moved = growth * q.astype(F32) - mwu[:, :, :DK]
        for c in range(chunks):
            if c == 0:
                query_ref[h, c] = moved[c]
                read_ref[h, c] = mwu[c, :, DK:]
                continue
            both = dot3(moved[c], carries[c - 1], 1, 1)
            query_ref[h, c] = both[:, :DK]
            read_ref[h, c] = mwu[c, :, DK:] + both[:, DK:]

    def join(h):
        pair_copy(h).wait_recv()

        @pl.when(chip < chips - 1)
        def _():
            own = own_map[h]
            other = sib_map[h].astype(F32)
            before = jnp.where(core == 0, own, other)
            after = jnp.where(core == 0, other, own)
            both = dot3(before, after[:DK], 1, 0)
            total[h, :DK] = both[:DK].astype(BF16)
            total[h, DK:] = (both[DK:] + after[DK:]).astype(BF16)

        for source in range(chips - 1):

            @pl.when(chip == source)
            def _():
                for dest in range(chips - 1, source, -1):
                    to_chip(h, source, dest).start()

    def enter(h):
        @pl.when(chip == 0)
        def _():
            prev[h] = jnp.zeros((DV, DK), F32)

        for source in range(chips - 1):

            @pl.when(chip > source)
            def _():
                to_chip(h, source, chip).wait_recv()
                if source == 0:
                    prev[h] = got[0, h, DK:].astype(F32)
                else:
                    prev[h] = dot2(prev[h], got[source, h, :DK], 1, 0) + got[
                        source, h, DK:
                    ].astype(F32)

        @pl.when(core == 1)
        def _():
            prev[h] = dot2(prev[h], sib_map[h, :DK], 1, 0) + sib_map[h, DK:].astype(F32)

    def place(h, source):
        return out_ref.at[:, pl.ds(pl.multiple_of((source * heads + h) * DV, DV), DV)]

    def outgoing(h, i):
        dest = lax.rem(z + i, streams)
        return remote(
            mixed.at[h, dest], place(h, z), out_send.at[dest, h], out_recv.at[z, h], (t, dest)
        )

    def incoming(h, i):
        source = lax.rem(z + i, streams)
        return remote(
            mixed.at[h, source],
            place(h, source),
            out_send.at[source, h],
            out_recv.at[source, h],
            (t, source),
        )

    def own_out(h):
        return pltpu.make_async_copy(mixed.at[h, z], place(h, z), out_own.at[h])

    far = list(reversed(near))
    per = local // CHUNK

    def finish(h):
        state = prev[h]
        for i in far + [0]:
            dest = lax.rem(z + i, streams)
            for c in range(per):
                at = dest * per + c
                read = read_ref[h, at] + dot3(query_ref[h, at], state, 1, 1)
                readout = read.astype(BF16).astype(F32)
                scale = lax.rsqrt(jnp.mean(readout * readout, -1, keepdims=True) + 1e-06)
                mixed[h, dest, c * CHUNK : (c + 1) * CHUNK] = (
                    readout * scale * gain_ref[...]
                ).astype(BF16)
            if i == 0:
                own_out(h).start()
            else:
                outgoing(h, i).start()

    stages = (join, enter, finish)
    for h in range(heads + len(stages)):
        if h < heads:
            if h in late:
                pass_on(h)
            if h + 1 in late:
                spread(h + 1)
            arrived(h)
            compute(h)
        for n, run in enumerate(stages):
            at = h - n if h >= heads else h - n - 1
            if h >= heads:
                at = h - n - 1
            if 0 <= at < heads:
                run(at)

    for h in range(heads):
        own_out(h).wait()
        for i in far:
            incoming(h, i).wait_recv()
    for h in range(heads):
        for i in far:
            outgoing(h, i).wait_send()
        pair_copy(h).wait_send()
        for source in range(chips - 1):

            @pl.when(chip == source)
            def _():
                for dest in range(chips - 1, source, -1):
                    to_chip(h, source, dest).wait_send()

    for u in range(heads):

        def sent():
            for n in near:
                cross(u, n).wait_send()
                s = lax.rem(z + n, streams)
                for j in range(chips):
                    plane(u, j, s).wait_send()

        only(is_sender, sent)
        for i in range(origins):
            if i == 0:
                if paired:
                    continue
                cond = active & (chip != base)
            else:
                cond = active

            def passed():
                for n in near:
                    relay(u, i, lax.rem(z + n, streams)).wait_send()

            only(cond, passed)
    for i in near:
        gate_out(i).wait_send()
        gate_on(i).wait_send()
    for k in range(streams):
        for p in range(PIECES):

            @pl.when((z >= k) & (z < streams - 1))
            def _():
                line(z - k, p, True, k == 0).wait_send()

            @pl.when((z + k < streams) & (z > 0))
            def _():
                line(z + k, p, False, k == 0).wait_send()


def shards(
    tokens, w_query, w_key, w_value, decay_proj, beta_proj, decay_rate, beta_bias, norm_gain
):
    streams = lax.axis_size("stream")
    places = lax.axis_size("tm")
    heads = HEADS // streams
    depth = w_query.shape[0]
    senders = min(places, depth // 16)
    share = depth // senders
    local, features = tokens.shape
    rows = streams * local
    chunks = rows // CHUNK
    chips = places // 2
    any_space = pl.BlockSpec(memory_space=pl.ANY)
    vmem = pl.BlockSpec(memory_space=pltpu.VMEM)
    dma = pltpu.SemaphoreType.DMA
    return pl.pallas_call(
        functools.partial(layer_kernel, streams, places, heads, senders),
        out_shape=jax.ShapeDtypeStruct((local, HEADS * DV), BF16),
        in_specs=[any_space] * 6 + [vmem] * 3,
        out_specs=any_space,
        scratch_shapes=[
            pltpu.VMEM((streams, local, features), BF16),
            pltpu.VMEM((heads, streams, depth, WIDTH), BF16),
            pltpu.VMEM((streams, heads, share, WIDTH), BF16),
            pltpu.VMEM((2, streams, HEADS, depth), BF16),
            pltpu.VMEM((chunks, CHUNK, HEADS), F32),
            pltpu.VMEM((chunks, HEADS, CHUNK), F32),
            pltpu.VMEM((chunks, CHUNK, HEADS), F32),
            pltpu.VMEM((heads, chunks, CHUNK, DV), F32),
            pltpu.VMEM((heads, chunks, CHUNK, DK), F32),
            pltpu.VMEM((heads, DK + DV, DK), F32),
            pltpu.VMEM((heads, DK + DV, DK), BF16),
            pltpu.VMEM((heads, DK + DV, DK), BF16),
            pltpu.VMEM((heads, DK + DV, DK), BF16),
            pltpu.VMEM((chips, heads, DK + DV, DK), BF16),
            pltpu.VMEM((heads, DV, DK), F32),
            pltpu.VMEM((heads, streams, local, DV), BF16),
            dma((streams, heads)),
            dma((heads,)),
            dma((2,)),
            dma((1,)),
            dma((streams,)),
            dma((streams,)),
            dma((streams,)),
            dma((streams,)),
            dma((streams, PIECES)),
            dma((streams, PIECES)),
            dma((streams, PIECES)),
            dma((streams, heads)),
            dma((streams, heads)),
            dma((chips, streams, heads)),
            dma((max(senders, chips), streams, heads)),
            dma((senders, streams, heads)),
            dma((heads,)),
            dma((heads,)),
            dma((chips, heads)),
            dma((chips, heads)),
            dma((streams, heads)),
            dma((streams, heads)),
            dma((heads,)),
        ],
        compiler_params=pltpu.CompilerParams(collective_id=0, has_side_effects=True),
    )(
        tokens,
        w_query,
        w_key,
        w_value,
        decay_proj.T,
        beta_proj.T,
        decay_rate[None],
        beta_bias[None],
        norm_gain[None],
    )


def solution(mesh):
    return jax.shard_map(
        shards,
        mesh=mesh,
        in_specs=(
            P(("tm", "stream"), None),
            P("stream", None),
            P("stream", None),
            P("stream", None),
            P("stream", None),
            P("stream", None),
            P(),
            P(),
            P(),
        ),
        out_specs=P(("tm", "stream"), None),
        check_vma=False,
    )
```

time: 113 us -> 100 us (0.88)
  Pallas kernels: 107 us -> 97.6 us
  local copies, waits for them, and re-layouts: 3.98 us -> 1.88 us
    pallas_call x3 -> x1, Pallas kernels: 107 us -> 97.6 us  [shards(): pl.pallas_call(functools.partial(layer_kernel, streams, places, heads, se...]
    broadcast_in_dim x1 -> x0, local copies, waits for them, and re-layouts: 1.29 us -> none  [shards(): bias = jnp.pad(beta_bias, (HEADS, LANES - 2 * HEADS))[None]]
where the time goes in v1:
time: 100 us; the launch traced here: 99.4 us
  Pallas kernels  97.6 us (98%)
  local copies, waits for them, and re-layouts  1.88 us (2%)
    pallas_call x1, Pallas kernels, shards(): pl.pallas_call(functools.partial(layer_kernel, streams, places, heads, se...  97.6 us

profile of v1, /device:TPU:4, one launch (start us, length us, event | category | flops | bytes accessed | tf_op | source)
XLA Modules:
  0.0 99.4 jit_solution(15490126233769192797)
XLA Ops:
  0.0 97.6 %shard_map.91 = bf16[128,2048]{1,0:T(8,128)(2,1)} custom-call(bf16[128,2048]{1,0:T(8,128)(2,1)} %tok_ref.1, bf16[512,2048]{1,0:T(8,128)(2,1)} %wq_ref.1, bf16[512,2048]{1,0:T(8,128)(2,1)} %wk_ref.1, bf16[512,2048]{1,0:T(8,128)(2,1)} %wv_ref.1, bf16[16,512]{1,0:T(8,128)(2,1)} %bitcast.5, bf16[16,512]{1,0:T(8,128)(2,1)} %bitcast.6, f32[1,16]{1,0:T(1,128)} %bitcast.7, ...), custom_call_target="tpu_custom_call" | custom-call | tf_op jit(solution)/shard_map/pallas_call | solution.py:645
  97.6 1.9 %copy.11 = bf16[128,2048]{1,0:T(8,128)(2,1)} copy(bf16[128,2048]{1,0:T(8,128)(2,1)} %shard_map.91) | data formatting | bytes 1048576

commit v2 on v1

v2 whole, which is shorter than its diff:
```python
import functools

import jax
import jax.numpy as jnp
from jax import lax
from jax.experimental import pallas as pl
from jax.experimental.pallas import tpu as pltpu
from jax.sharding import PartitionSpec as P

HEADS = 16
DK = 128
DV = 128
CHUNK = 128
PIECES = 4
GROUPS = 2
F32 = jnp.float32
BF16 = jnp.bfloat16


def halves(a):
    high = a.astype(BF16)
    return high, (a - high.astype(F32)).astype(BF16)


def contract(a, b, dims):
    return lax.dot_general(a, b, dims, preferred_element_type=F32)


def dot3(a, b, ca, cb, batch=0):
    ah, al = halves(a)
    bh, bl = halves(b)
    free = batch + (cb - batch + 1) % 2
    lead = tuple(range(batch))
    wide = jnp.concatenate([bh, bl], free)
    both = contract(
        jnp.concatenate([ah, al], ca),
        jnp.concatenate([wide, wide], cb),
        (((ca,), (cb,)), (lead, lead)),
    )
    half = both.shape[-1] // 2
    return both[..., :half] + both[..., half:]


def dot2(a, b, ca, cb):
    ah, al = halves(a)
    return contract(
        jnp.concatenate([ah, al], ca), jnp.concatenate([b, b], cb), (((ca,), (cb,)), ((), ()))
    )


def around(count):
    return sorted(range(1, count), key=lambda i: min(i, count - i))


def layer_kernel(
    streams,
    places,
    heads,
    senders,
    tok_ref,
    wq_ref,
    wk_ref,
    wv_ref,
    dec_ref,
    bet_ref,
    rate_ref,
    bias_ref,
    gain_ref,
    out_ref,
    x_ref,
    full,
    stage,
    gates,
    cum_row,
    step_ref,
    run_ref,
    read_ref,
    query_ref,
    sent_map,
    sib_map,
    total,
    got,
    prev,
    mixed,
    load_sem,
    own_sem,
    gate_load,
    tok_load,
    gate_send,
    gate_recv,
    gate_pass,
    gate_sib,
    right_sem,
    left_sem,
    tok_recv,
    cross_send,
    cross_recv,
    plane_send,
    plane_recv,
    pass_send,
    sib_recv,
    pair_send,
    pair_recv,
    chip_send,
    chip_recv,
    out_send,
    out_recv,
    out_own,
):
    t = lax.axis_index("tm")
    z = lax.axis_index("stream")
    chips = places // 2
    chip = t // 2
    core = t % 2
    sibling = chip * 2 + 1 - core
    depth = wq_ref.shape[0]
    share = depth // senders
    stride = places // senders
    step = max(stride // 2, 1)
    paired = stride == 1
    origins = senders // 2 if paired else senders
    base = chip // step * step
    local, features = tok_ref.shape
    part = local // PIECES
    near = around(streams)
    span = heads * DK
    groups = GROUPS if heads % GROUPS == 0 else 1
    each = heads // groups

    def remote(src, dst, send, recv, device):
        return pltpu.make_async_remote_copy(
            src_ref=src,
            dst_ref=dst,
            send_sem=send,
            recv_sem=recv,
            device_id=device,
            device_id_type=pl.DeviceIdType.MESH,
        )

    def drain(ref, sem):
        pltpu.make_async_copy(ref, ref, sem).wait()

    def only(cond, body):
        if cond is True:
            body()
        elif cond is not False:
            pl.when(cond)(body)

    is_sender = True if paired else (t % stride == 0)
    active = True if paired else (core == 0)
    mine = t // stride

    def slot(i):
        at = lax.rem(base + i * step, chips)
        return 2 * at + core if paired else at // step

    weights = (wq_ref, wk_ref, wv_ref)
    my_rows = pl.ds(pl.multiple_of(mine * share, share), share)

    def load_stage():
        for i in near:
            dest = lax.rem(z + i, streams)
            for j, ref in enumerate(weights):
                pltpu.make_async_copy(
                    ref.at[my_rows, pl.ds(pl.multiple_of(dest * span, span), span)],
                    stage.at[dest, :, pl.ds(j * span, span)],
                    load_sem.at[dest],
                ).start()

    only(is_sender, load_stage)
    pltpu.make_async_copy(dec_ref, gates.at[0, z], gate_load.at[0]).start()
    pltpu.make_async_copy(bet_ref, gates.at[1, z], gate_load.at[0]).start()
    own_tok = pltpu.make_async_copy(tok_ref, x_ref.at[z], tok_load.at[0])
    own_tok.start()
    for j, ref in enumerate(weights):
        pltpu.make_async_copy(
            ref.at[:, pl.ds(pl.multiple_of(z * span, span), span)],
            full.at[z, :, pl.ds(j * span, span)],
            own_sem.at[0],
        ).start()

    others = [lax.rem(chip + i, chips) * 2 + core for i in range(1, chips)]
    peers = [(t, lax.rem(z + i, streams)) for i in near]
    peers += [(sibling, z)] + [(o, z) for o in others]
    barrier = pltpu.get_barrier_semaphore()
    for peer in peers:
        pl.semaphore_signal(
            barrier, inc=1, device_id=peer, device_id_type=pl.DeviceIdType.MESH
        )
    pl.semaphore_wait(barrier, len(peers))

    def rows_of(k):
        return pl.ds(pl.multiple_of(k * share, share), share)

    def line(s, p, right, first):
        at = pl.ds(p * part, part)
        src = tok_ref.at[at] if first else x_ref.at[s, at]
        send = (right_sem if right else left_sem).at[s]
        return remote(
            src, x_ref.at[s, at], send, tok_recv.at[s, p], (t, z + 1 if right else z - 1)
        )

    def gate_out(i):
        dest = lax.rem(z + i, streams)
        here = gates.at[core, z]
        return remote(here, here, gate_send.at[0], gate_recv.at[z], (t, dest))

    def gate_in(i):
        s = lax.rem(z + i, streams)
        here = gates.at[core, s]
        return remote(here, here, gate_send.at[0], gate_recv.at[s], (t, s))

    def gate_on(i):
        s = lax.rem(z + i, streams)
        here = gates.at[core, s]
        return remote(here, here, gate_pass.at[0], gate_sib.at[0], (sibling, z))

    def cross(i):
        dest = lax.rem(z + i, streams)
        return remote(
            stage.at[dest], full.at[z, rows_of(mine)], cross_send.at[0], cross_recv.at[z], (t, dest)
        )

    def crossed(i):
        s = lax.rem(z + i, streams)
        return remote(
            stage.at[s], full.at[s, rows_of(mine)], cross_send.at[0], cross_recv.at[s], (t, s)
        )

    def plane(i, s):
        here = full.at[s, rows_of(mine)]
        return remote(
            here, here, plane_send.at[i], plane_recv.at[mine, s], (others[i - 1], z)
        )

    def beside(k, s):
        here = full.at[s, rows_of(k)]
        return remote(here, here, pass_send.at[0], sib_recv.at[0], (sibling, z))

    def landed(k, s):
        here = full.at[s, rows_of(k)]
        return remote(here, here, plane_send.at[0], plane_recv.at[k, s], (others[0], z))

    def token_step(k, pieces):
        for p in pieces:

            @pl.when(z >= k)
            def _():
                line(z - k, p, True, False).wait_recv()

                @pl.when(z < streams - 1)
                def _():
                    line(z - k, p, True, False).start()

            @pl.when(z + k < streams)
            def _():
                line(z + k, p, False, False).wait_recv()

                @pl.when(z > 0)
                def _():
                    line(z + k, p, False, False).start()

    def send_shares():
        for i in near:
            drain(stage.at[lax.rem(z + i, streams)], load_sem.at[lax.rem(z + i, streams)])
            cross(i).start()

    only(is_sender, send_shares)
    drain(gates.at[:, z], gate_load.at[0])
    for i in near:
        gate_out(i).start()
    for p in range(PIECES):

        @pl.when(z < streams - 1)
        def _():
            line(z, p, True, True).start()

        @pl.when(z > 0)
        def _():
            line(z, p, False, True).start()

    def spread():
        for i in near:
            s = lax.rem(z + i, streams)
            crossed(i).wait_recv()
            for j in range(1, chips):
                plane(j, s).start()
            beside(mine, s).start()

    only(is_sender, spread)
    for i in near:
        gate_in(i).wait_recv()
        gate_on(i).start()

    def pass_on(i):
        if i == 0:
            if paired:
                return
            cond = active & (chip != base)
        else:
            cond = active
        k = slot(i)

        def body():
            for n in near:
                s = lax.rem(z + n, streams)
                landed(k, s).wait_recv()
                beside(k, s).start()

        only(cond, body)

    for p in range(PIECES):
        token_step(1, [p])
        for i in range(origins * p // PIECES, origins * (p + 1) // PIECES):
            pass_on(i)
    own_tok.wait()
    drain(full.at[z], own_sem.at[0])
    drain(gates.at[0, pl.ds(0, streams - 1)], gate_sib.at[0])
    only(
        True if paired else core == 1,
        lambda: drain(full.at[pl.ds(0, streams - 1), pl.ds(0, origins * share)], sib_recv.at[0]),
    )

    row_at = lax.broadcasted_iota(jnp.int32, (CHUNK, CHUNK), 0)
    col_at = lax.broadcasted_iota(jnp.int32, (CHUNK, CHUNK), 1)
    low = row_at >= col_at
    strict = row_at > col_at
    eye = jnp.where(row_at == col_at, 1.0, 0.0)
    lower_ones = jnp.where(low, 1.0, 0.0).astype(BF16)
    lane = lax.broadcasted_iota(jnp.int32, (CHUNK, HEADS), 1)

    def turn(n):
        fewer = jnp.minimum(z, streams - 1 - z)
        left = z * 2 >= streams
        both = n <= 2 * fewer
        k = jnp.where(both, (n + 1) // 2, n - fewer)
        leftward = jnp.where(both, jnp.where(left, n % 2 == 0, n % 2 == 1), left)
        at = jnp.where(leftward, z - k, z + k)
        return (z, None) if n == 0 else (at, leftward)

    def columns(a, first):
        picked = [
            jnp.sum(jnp.where(lane == z * heads + h, a, 0.0), -1, keepdims=True)
            for h in range(heads)
        ]
        return jnp.stack(picked)

    def split(a):
        return jnp.stack([a[:, h * DK : (h + 1) * DK] for h in range(heads)])

    def process(n):
        at, leftward = turn(n)
        x = x_ref[at]
        sums = None
        for s in range(streams):
            g2 = gates[:, s].reshape(2 * HEADS, depth)
            term = contract(x[:, s * depth : (s + 1) * depth], g2, (((1,), (1,)), ((), ())))
            sums = term if sums is None else sums + term
        first = sums[:, :HEADS]
        soft = jnp.maximum(first, 0.0) + jnp.log1p(jnp.exp(-jnp.abs(first)))
        decay = (-rate_ref[...] * soft).astype(BF16)
        beta = (1.0 / (1.0 + jnp.exp(-(sums[:, HEADS:] + bias_ref[...])))).astype(BF16).astype(F32)
        cum = contract(lower_ones, decay, (((1,), (0,)), ((), ())))
        cum_row[...] = cum.T
        g = columns(cum, 0)
        b = columns(beta, 0)
        g_row = jnp.stack([cum_row[pl.ds(z * heads + h, 1), :] for h in range(heads)])

        def project(j):
            w = full[:, :, j * span : (j + 1) * span].reshape(streams * depth, span)
            return split(contract(x, w, (((1,), (0,)), ((), ()))))

        raw_k = project(1)
        k = (raw_k * lax.rsqrt(jnp.sum(raw_k * raw_k, -1, keepdims=True) + 1e-06)).astype(BF16)
        raw_q = project(0)
        q = (
            raw_q * lax.rsqrt(jnp.sum(raw_q * raw_q, -1, keepdims=True) + 1e-06) * DK ** (-0.5)
        ).astype(BF16)
        v = project(2).astype(BF16).astype(F32)
        g_last = g[:, CHUNK - 1 :, :]
        growth = jnp.exp(g)
        tail = jnp.exp(g_last - g)
        whole = jnp.exp(g_last)

        pair = contract(jnp.concatenate([k, q], 1), k, (((2,), (2,)), ((0,), (0,))))
        spread_ = jnp.exp(jnp.where(low[None], g - g_row, 0.0))
        lmat = jnp.where(strict[None], b * spread_ * pair[:, :CHUNK], 0.0)
        mmat = jnp.where(low[None], spread_ * pair[:, CHUNK:], 0.0)

        inverse = None
        size = 1
        while size < CHUNK:
            inside = (row_at // (2 * size) == col_at // (2 * size)) & (
                row_at // size != col_at // size
            )
            off = jnp.where(inside[None], lmat, 0.0)
            if inverse is None:
                inverse = eye[None] - off
            else:
                inverse = inverse - dot3(inverse, dot3(off, inverse, 2, 1, 1), 2, 1, 1)
            size *= 2

        kf = k.astype(F32)
        right = jnp.concatenate([(b * growth) * kf, b * v], 2)
        wu = dot3(inverse, right, 2, 1, 1)
        jumps = dot3(jnp.swapaxes(wu, 1, 2), tail * kf, 2, 1, 1)
        step_map = jnp.concatenate([whole * eye[None] - jumps[:, :DK], jumps[:, DK:]], 1)
        step_ref[at] = step_map
        if n == 0:
            run = step_map
        else:
            run = run_ref[...]
            before = jnp.where(leftward, step_map, run)
            after = jnp.where(leftward, run, step_map)
            run = join_maps(before, after)
        if n < streams - 1:
            run_ref[...] = run
        else:
            sent_map[...] = run.astype(BF16)
            for gr in range(groups):
                pair_copy(gr).start()
            run_ref[...] = run
        mwu = dot3(mmat, wu, 2, 1, 1)
        query_ref[at] = growth * q.astype(F32) - mwu[:, :, :DK]
        read_ref[at] = mwu[:, :, DK:]

    def join_maps(before, after):
        both = dot3(before, after[:, :DK], 2, 1, 1)
        return jnp.concatenate([both[:, :DK], both[:, DK:] + after[:, DK:]], 1)

    def group(gr):
        return pl.ds(gr * each, each)

    def pair_copy(gr):
        return remote(
            sent_map.at[group(gr)],
            sib_map.at[group(gr)],
            pair_send.at[gr],
            pair_recv.at[gr],
            (sibling, z),
        )

    def to_chip(gr, source, dest):
        src, dst = total.at[group(gr)], got.at[source, group(gr)]
        if source == 0:
            src = total.at[group(gr), pl.ds(DK, DV)]
            dst = got.at[0, group(gr), pl.ds(DK, DV)]
        return remote(
            src, dst, chip_send.at[dest, gr], chip_recv.at[source, gr], (dest * 2 + core, z)
        )

    for n in range(streams):
        process(n)
        if n == 0 and streams > 2:
            token_step(2, range(PIECES // 2))
        elif n == 1 and streams > 2:
            token_step(2, range(PIECES // 2, PIECES))
        elif 2 <= n < streams - 1:
            token_step(n + 1, range(PIECES))

    def join(gr):
        pair_copy(gr).wait_recv()

        @pl.when(chip < chips - 1)
        def _():
            own = run_ref[gr * each : (gr + 1) * each]
            other = sib_map[gr * each : (gr + 1) * each].astype(F32)
            before = jnp.where(core == 0, own, other)
            after = jnp.where(core == 0, other, own)
            total[gr * each : (gr + 1) * each] = join_maps(before, after).astype(BF16)

        for source in range(chips - 1):

            @pl.when(chip == source)
            def _():
                for dest in range(chips - 1, source, -1):
                    to_chip(gr, source, dest).start()

    def prefixes():
        carry = step_ref[0]
        for c in range(1, streams):
            both = dot3(query_ref[c], carry, 2, 2, 1)
            query_ref[c] = both[:, :, :DK]
            read_ref[c] = read_ref[c] + both[:, :, DK:]
            if c < streams - 1:
                carry = join_maps(carry, step_ref[c])

    def enter(gr):
        hs = range(gr * each, (gr + 1) * each)

        @pl.when(chip == 0)
        def _():
            for h in hs:
                prev[h] = jnp.zeros((DV, DK), F32)

        for source in range(chips - 1):

            @pl.when(chip > source)
            def _():
                to_chip(gr, source, chip).wait_recv()
                for h in hs:
                    if source == 0:
                        prev[h] = got[0, h, DK:].astype(F32)
                    else:
                        prev[h] = dot2(prev[h], got[source, h, :DK], 1, 0) + got[
                            source, h, DK:
                        ].astype(F32)

        @pl.when(core == 1)
        def _():
            for h in hs:
                prev[h] = dot2(prev[h], sib_map[h, :DK], 1, 0) + sib_map[h, DK:].astype(F32)

    wide = each * DV

    def spot(gr, source):
        return out_ref.at[
            :, pl.ds(pl.multiple_of(source * span + gr * wide, wide), wide)
        ]

    def outgoing(gr, i):
        dest = lax.rem(z + i, streams)
        return remote(
            mixed.at[gr, dest], spot(gr, z), out_send.at[dest, gr], out_recv.at[z, gr], (t, dest)
        )

    def incoming(gr, i):
        source = lax.rem(z + i, streams)
        return remote(
            mixed.at[gr, source],
            spot(gr, source),
            out_send.at[source, gr],
            out_recv.at[source, gr],
            (t, source),
        )

    def own_out(gr):
        return pltpu.make_async_copy(mixed.at[gr, z], spot(gr, z), out_own.at[gr])

    far = list(reversed(near))

    def finish(gr):
        for i in far + [0]:
            dest = lax.rem(z + i, streams)
            for n in range(each):
                h = gr * each + n
                read = read_ref[dest, h] + dot3(query_ref[dest, h], prev[h], 1, 1)
                readout = read.astype(BF16).astype(F32)
                scale = lax.rsqrt(jnp.mean(readout * readout, -1, keepdims=True) + 1e-06)
                mixed[gr, dest, :, n * DV : (n + 1) * DV] = (
                    readout * scale * gain_ref[...]
                ).astype(BF16)
            if i == 0:
                own_out(gr).start()
            else:
                outgoing(gr, i).start()

    for gr in range(groups):
        join(gr)
    prefixes()
    for gr in range(groups):
        enter(gr)
        finish(gr)

    for gr in range(groups):
        own_out(gr).wait()
        for i in far:
            incoming(gr, i).wait_recv()
    for gr in range(groups):
        for i in far:
            outgoing(gr, i).wait_send()
        pair_copy(gr).wait_send()
        for source in range(chips - 1):

            @pl.when(chip == source)
            def _():
                for dest in range(chips - 1, source, -1):
                    to_chip(gr, source, dest).wait_send()

    def sent():
        drain(stage.at[pl.ds(0, streams - 1)], cross_send.at[0])
        for i in range(1, chips):
            drain(full.at[pl.ds(0, streams - 1), pl.ds(0, share)], plane_send.at[i])

    only(is_sender, sent)
    if paired:
        drain(full.at[pl.ds(0, streams - 1), pl.ds(0, origins * share)], pass_send.at[0])
    else:

        @pl.when(core == 0)
        def _():
            drain(full.at[pl.ds(0, streams - 1), pl.ds(0, origins * share)], pass_send.at[0])

    drain(gates.at[0, pl.ds(0, streams - 1)], gate_send.at[0])
    drain(gates.at[0, pl.ds(0, streams - 1)], gate_pass.at[0])
    for k in range(streams):

        @pl.when((z >= k) & (z < streams - 1))
        def _():
            drain(x_ref.at[z - k], right_sem.at[z - k])

        @pl.when((z + k < streams) & (z > 0))
        def _():
            drain(x_ref.at[z + k], left_sem.at[z + k])


def shards(
    tokens, w_query, w_key, w_value, decay_proj, beta_proj, decay_rate, beta_bias, norm_gain
):
    streams = lax.axis_size("stream")
    places = lax.axis_size("tm")
    heads = HEADS // streams
    depth = w_query.shape[0]
    senders = min(places, depth // 16)
    share = depth // senders
    local, features = tokens.shape
    chips = places // 2
    width = 3 * heads * DK
    groups = GROUPS if heads % GROUPS == 0 else 1
    any_space = pl.BlockSpec(memory_space=pl.ANY)
    vmem = pl.BlockSpec(memory_space=pltpu.VMEM)
    dma = pltpu.SemaphoreType.DMA
    return pl.pallas_call(
        functools.partial(layer_kernel, streams, places, heads, senders),
        out_shape=jax.ShapeDtypeStruct((local, HEADS * DV), BF16),
        in_specs=[any_space] * 6 + [vmem] * 3,
        out_specs=any_space,
        scratch_shapes=[
            pltpu.VMEM((streams, local, features), BF16),
            pltpu.VMEM((streams, depth, width), BF16),
            pltpu.VMEM((streams, share, width), BF16),
            pltpu.VMEM((2, streams, HEADS, depth), BF16),
            pltpu.VMEM((HEADS, CHUNK), F32),
            pltpu.VMEM((streams, heads, DK + DV, DK), F32),
            pltpu.VMEM((heads, DK + DV, DK), F32),
            pltpu.VMEM((streams, heads, CHUNK, DV), F32),
            pltpu.VMEM((streams, heads, CHUNK, DK), F32),
            pltpu.VMEM((heads, DK + DV, DK), BF16),
            pltpu.VMEM((heads, DK + DV, DK), BF16),
            pltpu.VMEM((heads, DK + DV, DK), BF16),
            pltpu.VMEM((chips, heads, DK + DV, DK), BF16),
            pltpu.VMEM((heads, DV, DK), F32),
            pltpu.VMEM((groups, streams, local, heads // groups * DV), BF16),
            dma((streams,)),
            dma((1,)),
            dma((1,)),
            dma((1,)),
            dma((1,)),
            dma((streams,)),
            dma((1,)),
            dma((1,)),
            dma((streams,)),
            dma((streams,)),
            dma((streams, PIECES)),
            dma((1,)),
            dma((streams,)),
            dma((chips,)),
            dma((senders, streams)),
            dma((1,)),
            dma((1,)),
            dma((groups,)),
            dma((groups,)),
            dma((chips, groups)),
            dma((chips, groups)),
            dma((streams, groups)),
            dma((streams, groups)),
            dma((groups,)),
        ],
        compiler_params=pltpu.CompilerParams(collective_id=0, has_side_effects=True),
    )(
        tokens,
        w_query,
        w_key,
        w_value,
        decay_proj.T,
        beta_proj.T,
        decay_rate[None],
        beta_bias[None],
        norm_gain[None],
    )


def solution(mesh):
    return jax.shard_map(
        shards,
        mesh=mesh,
        in_specs=(
            P(("tm", "stream"), None),
            P("stream", None),
            P("stream", None),
            P("stream", None),
            P("stream", None),
            P("stream", None),
            P(),
            P(),
            P(),
        ),
        out_specs=P(("tm", "stream"), None),
        check_vma=False,
    )
```

time: 100 us -> 87.8 us (0.88)
  Pallas kernels: 97.6 us -> 85.8 us
    pallas_call x1, Pallas kernels: 97.6 us -> 85.8 us  [shards(): pl.pallas_call(functools.partial(layer_kernel, streams, places, heads, se...]
where the time goes in v2:
time: 87.8 us; the launch traced here: 87.7 us
  Pallas kernels  85.8 us (98%)
  local copies, waits for them, and re-layouts  1.88 us (2%)
    pallas_call x1, Pallas kernels, shards(): pl.pallas_call(functools.partial(layer_kernel, streams, places, heads, se...  85.8 us
    unnamed x1, local copies, waits for them, and re-layouts  1.88 us

profile of v2, /device:TPU:4, one launch (start us, length us, event | category | flops | bytes accessed | tf_op | source)
XLA Modules:
  0.0 87.7 jit_solution(2423124599399636106)
XLA Ops:
  0.0 85.8 %shard_map.91 = bf16[128,2048]{1,0:T(8,128)(2,1)} custom-call(bf16[128,2048]{1,0:T(8,128)(2,1)} %tok_ref.1, bf16[512,2048]{1,0:T(8,128)(2,1)} %wq_ref.1, bf16[512,2048]{1,0:T(8,128)(2,1)} %wk_ref.1, bf16[512,2048]{1,0:T(8,128)(2,1)} %wv_ref.1, bf16[16,512]{1,0:T(8,128)(2,1)} %bitcast.5, bf16[16,512]{1,0:T(8,128)(2,1)} %bitcast.6, f32[1,16]{1,0:T(1,128)} %bitcast.7, ...), custom_call_target="tpu_custom_call" | custom-call | tf_op jit(solution)/shard_map/pallas_call | solution.py:623
  85.8 1.9 %copy.11 = bf16[128,2048]{1,0:T(8,128)(2,1)} copy(bf16[128,2048]{1,0:T(8,128)(2,1)} %shard_map.91) | data formatting | bytes 1048576

commit v3 on v2

--- a/solution.py
+++ b/solution.py
@@ -12,7 +12,6 @@
 DV = 128
 CHUNK = 128
 PIECES = 4
-GROUPS = 2
 F32 = jnp.float32
 BF16 = jnp.bfloat16
 
@@ -81,6 +80,7 @@
     total,
     got,
     prev,
+    state,
     mixed,
     load_sem,
     own_sem,
@@ -103,6 +103,8 @@
     pair_recv,
     chip_send,
     chip_recv,
+    back_send,
+    back_recv,
     out_send,
     out_recv,
     out_own,
@@ -124,8 +126,8 @@
     part = local // PIECES
     near = around(streams)
     span = heads * DK
-    groups = GROUPS if heads % GROUPS == 0 else 1
-    each = heads // groups
+    halved = heads % 2 == 0
+    each = heads // 2 if halved else heads
 
     def remote(src, dst, send, recv, device):
         return pltpu.make_async_remote_copy(
@@ -309,10 +311,9 @@
 
         only(cond, body)
 
-    for p in range(PIECES):
-        token_step(1, [p])
-        for i in range(origins * p // PIECES, origins * (p + 1) // PIECES):
-            pass_on(i)
+    token_step(1, range(PIECES))
+    for i in range(origins):
+        pass_on(i)
     own_tok.wait()
     drain(full.at[z], own_sem.at[0])
     drain(gates.at[0, pl.ds(0, streams - 1)], gate_sib.at[0])
@@ -417,37 +418,50 @@
             run_ref[...] = run
         else:
             sent_map[...] = run.astype(BF16)
-            for gr in range(groups):
-                pair_copy(gr).start()
+            give(0).start()
+            give_rest(lambda copy: copy.start())
             run_ref[...] = run
         mwu = dot3(mmat, wu, 2, 1, 1)
-        query_ref[at] = growth * q.astype(F32) - mwu[:, :, :DK]
-        read_ref[at] = mwu[:, :, DK:]
+        query_ref[:, at] = growth * q.astype(F32) - mwu[:, :, :DK]
+        read_ref[:, at] = mwu[:, :, DK:]
 
     def join_maps(before, after):
         both = dot3(before, after[:, :DK], 2, 1, 1)
         return jnp.concatenate([both[:, :DK], both[:, DK:] + after[:, DK:]], 1)
 
-    def group(gr):
-        return pl.ds(gr * each, each)
-
-    def pair_copy(gr):
+    mine_at = core * each if halved else 0
+    theirs_at = (1 - core) * each if halved else 0
+
+    def give(which):
+        at = pl.ds(theirs_at if which == 0 else mine_at, each)
         return remote(
-            sent_map.at[group(gr)],
-            sib_map.at[group(gr)],
-            pair_send.at[gr],
-            pair_recv.at[gr],
-            (sibling, z),
-        )
-
-    def to_chip(gr, source, dest):
-        src, dst = total.at[group(gr)], got.at[source, group(gr)]
+            sent_map.at[at], sib_map.at[at], pair_send.at[which], pair_recv.at[which], (sibling, z)
+        )
+
+    def taken(which):
+        at = pl.ds(mine_at if which == 0 else theirs_at, each)
+        return remote(
+            sent_map.at[at], sib_map.at[at], pair_send.at[which], pair_recv.at[which], (sibling, z)
+        )
+
+    def give_rest(act):
+        if halved:
+
+            @pl.when(core == 0)
+            def _():
+                act(give(1))
+
+    def to_chip(n, source, dest):
+        src, dst = total.at[n], got.at[source, n]
         if source == 0:
-            src = total.at[group(gr), pl.ds(DK, DV)]
-            dst = got.at[0, group(gr), pl.ds(DK, DV)]
+            src, dst = total.at[n, pl.ds(DK, DV)], got.at[0, n, pl.ds(DK, DV)]
         return remote(
-            src, dst, chip_send.at[dest, gr], chip_recv.at[source, gr], (dest * 2 + core, z)
-        )
+            src, dst, chip_send.at[dest, n], chip_recv.at[source, n], (dest * 2 + core, z)
+        )
+
+    def back(n, start):
+        here = prev.at[start + n]
+        return remote(here, here, back_send.at[n], back_recv.at[n], (sibling, z))
 
     for n in range(streams):
         process(n)
@@ -458,124 +472,139 @@
         elif 2 <= n < streams - 1:
             token_step(n + 1, range(PIECES))
 
-    def join(gr):
-        pair_copy(gr).wait_recv()
+    def carries():
+        for c in range(1, streams - 1):
+            step_ref[c] = join_maps(step_ref[c - 1], step_ref[c])
+
+    def join():
+        taken(0).wait_recv()
 
         @pl.when(chip < chips - 1)
         def _():
-            own = run_ref[gr * each : (gr + 1) * each]
-            other = sib_map[gr * each : (gr + 1) * each].astype(F32)
+            at = pl.ds(mine_at, each)
+            own = run_ref[at]
+            other = sib_map[at].astype(F32)
             before = jnp.where(core == 0, own, other)
             after = jnp.where(core == 0, other, own)
-            total[gr * each : (gr + 1) * each] = join_maps(before, after).astype(BF16)
-
+            total[...] = join_maps(before, after).astype(BF16)
+
+        for source in range(chips - 1):
+
+            @pl.when(chip == source)
+            def _():
+                for n in range(each):
+                    for dest in range(chips - 1, source, -1):
+                        to_chip(n, source, dest).start()
+
+    def prefixes():
+        for c in range(1, streams):
+            both = dot3(query_ref[:, c], step_ref[c - 1], 2, 2, 1)
+            query_ref[:, c] = both[:, :, :DK]
+            read_ref[:, c] = read_ref[:, c] + both[:, :, DK:]
+
+    def enter(n):
+        h = mine_at + n
+
+        @pl.when(chip == 0)
+        def _():
+            prev[h] = jnp.zeros((DV, DK), F32)
+
+        for source in range(chips - 1):
+
+            @pl.when(chip > source)
+            def _():
+                to_chip(n, source, chip).wait_recv()
+                if source == 0:
+                    prev[h] = got[0, n, DK:].astype(F32)
+                else:
+                    prev[h] = dot2(prev[h], got[source, n, :DK], 1, 0) + got[
+                        source, n, DK:
+                    ].astype(F32)
+
+        if halved:
+
+            @pl.when(chip > 0)
+            def _():
+                back(n, mine_at).start()
+
+    def hear(n):
+        h = theirs_at + n
+
+        @pl.when(chip == 0)
+        def _():
+            prev[h] = jnp.zeros((DV, DK), F32)
+
+        @pl.when(chip > 0)
+        def _():
+            back(n, theirs_at).wait_recv()
+
+    def spot(h, source):
+        at = pl.multiple_of((source * heads + h) * DV, DV)
+        return out_ref.at[:, pl.ds(at, DV)]
+
+    def outgoing(h, i):
+        dest = lax.rem(z + i, streams)
+        return remote(
+            mixed.at[h, dest], spot(h, z), out_send.at[0], out_recv.at[z], (t, dest)
+        )
+
+    def own_out(h):
+        return pltpu.make_async_copy(mixed.at[h, z], spot(h, z), out_own.at[0])
+
+    far = list(reversed(near))
+
+    def finish(h):
+        carried = prev[h]
+        state[...] = carried
+
+        @pl.when(core == 1)
+        def _():
+            state[...] = dot2(carried, sib_map[h, :DK], 1, 0) + sib_map[h, DK:].astype(F32)
+
+        reads = dot3(query_ref[h].reshape(streams * local, DK), state[...], 1, 1)
+        read = read_ref[h].reshape(streams * local, DV) + reads
+        readout = read.astype(BF16).astype(F32)
+        scale = lax.rsqrt(jnp.mean(readout * readout, -1, keepdims=True) + 1e-06)
+        mixed[h] = (readout * scale * gain_ref[...]).astype(BF16).reshape(streams, local, DV)
+        for i in far:
+            outgoing(h, i).start()
+        own_out(h).start()
+
+    carries()
+    join()
+    prefixes()
+    for n in range(each):
+        enter(n)
+        finish(mine_at + n)
+    if halved:
+
+        @pl.when(core == 1)
+        def _():
+            taken(1).wait_recv()
+
+        for n in range(each):
+            hear(n)
+            finish(theirs_at + n)
+
+    drain(mixed.at[:, 0], out_own.at[0])
+    for i in far:
+        drain(mixed.at[:, 0], out_recv.at[lax.rem(z + i, streams)])
+    drain(mixed.at[:, pl.ds(0, streams - 1)], out_send.at[0])
+    give(0).wait_send()
+    give_rest(lambda copy: copy.wait_send())
+    for n in range(each):
         for source in range(chips - 1):
 
             @pl.when(chip == source)
             def _():
                 for dest in range(chips - 1, source, -1):
-                    to_chip(gr, source, dest).start()
-
-    def prefixes():
-        carry = step_ref[0]
-        for c in range(1, streams):
-            both = dot3(query_ref[c], carry, 2, 2, 1)
-            query_ref[c] = both[:, :, :DK]
-            read_ref[c] = read_ref[c] + both[:, :, DK:]
-            if c < streams - 1:
-                carry = join_maps(carry, step_ref[c])
-
-    def enter(gr):
-        hs = range(gr * each, (gr + 1) * each)
-
-        @pl.when(chip == 0)
-        def _():
-            for h in hs:
-                prev[h] = jnp.zeros((DV, DK), F32)
-
-        for source in range(chips - 1):
-
-            @pl.when(chip > source)
+                    to_chip(n, source, dest).wait_send()
+
+        if halved:
+
+            @pl.when(chip > 0)
             def _():
-                to_chip(gr, source, chip).wait_recv()
-                for h in hs:
-                    if source == 0:
-                        prev[h] = got[0, h, DK:].astype(F32)
-                    else:
-                        prev[h] = dot2(prev[h], got[source, h, :DK], 1, 0) + got[
-                            source, h, DK:
-                        ].astype(F32)
-
-        @pl.when(core == 1)
-        def _():
-            for h in hs:
-                prev[h] = dot2(prev[h], sib_map[h, :DK], 1, 0) + sib_map[h, DK:].astype(F32)
-
-    wide = each * DV
-
-    def spot(gr, source):
-        return out_ref.at[
-            :, pl.ds(pl.multiple_of(source * span + gr * wide, wide), wide)
-        ]
-
-    def outgoing(gr, i):
-        dest = lax.rem(z + i, streams)
-        return remote(
-            mixed.at[gr, dest], spot(gr, z), out_send.at[dest, gr], out_recv.at[z, gr], (t, dest)
-        )
-
-    def incoming(gr, i):
-        source = lax.rem(z + i, streams)
-        return remote(
-            mixed.at[gr, source],
-            spot(gr, source),
-            out_send.at[source, gr],
-            out_recv.at[source, gr],
-            (t, source),
-        )
-
-    def own_out(gr):
-        return pltpu.make_async_copy(mixed.at[gr, z], spot(gr, z), out_own.at[gr])
-
-    far = list(reversed(near))
-
-    def finish(gr):
-        for i in far + [0]:
-            dest = lax.rem(z + i, streams)
-            for n in range(each):
-                h = gr * each + n
-                read = read_ref[dest, h] + dot3(query_ref[dest, h], prev[h], 1, 1)
-                readout = read.astype(BF16).astype(F32)
-                scale = lax.rsqrt(jnp.mean(readout * readout, -1, keepdims=True) + 1e-06)
-                mixed[gr, dest, :, n * DV : (n + 1) * DV] = (
-                    readout * scale * gain_ref[...]
-                ).astype(BF16)
-            if i == 0:
-                own_out(gr).start()
-            else:
-                outgoing(gr, i).start()
-
-    for gr in range(groups):
-        join(gr)
-    prefixes()
-    for gr in range(groups):
-        enter(gr)
-        finish(gr)
-
-    for gr in range(groups):
-        own_out(gr).wait()
-        for i in far:
-            incoming(gr, i).wait_recv()
-    for gr in range(groups):
-        for i in far:
-            outgoing(gr, i).wait_send()
-        pair_copy(gr).wait_send()
-        for source in range(chips - 1):
-
-            @pl.when(chip == source)
-            def _():
-                for dest in range(chips - 1, source, -1):
-                    to_chip(gr, source, dest).wait_send()
+                back(n, mine_at).wait_send()
 
     def sent():
         drain(stage.at[pl.ds(0, streams - 1)], cross_send.at[0])
@@ -616,7 +645,7 @@
     local, features = tokens.shape
     chips = places // 2
     width = 3 * heads * DK
-    groups = GROUPS if heads % GROUPS == 0 else 1
+    each = heads // 2 if heads % 2 == 0 else heads
     any_space = pl.BlockSpec(memory_space=pl.ANY)
     vmem = pl.BlockSpec(memory_space=pltpu.VMEM)
     dma = pltpu.SemaphoreType.DMA
@@ -633,14 +662,15 @@
             pltpu.VMEM((HEADS, CHUNK), F32),
             pltpu.VMEM((streams, heads, DK + DV, DK), F32),
             pltpu.VMEM((heads, DK + DV, DK), F32),
-            pltpu.VMEM((streams, heads, CHUNK, DV), F32),
-            pltpu.VMEM((streams, heads, CHUNK, DK), F32),
+            pltpu.VMEM((heads, streams, CHUNK, DV), F32),
+            pltpu.VMEM((heads, streams, CHUNK, DK), F32),
             pltpu.VMEM((heads, DK + DV, DK), BF16),
             pltpu.VMEM((heads, DK + DV, DK), BF16),
-            pltpu.VMEM((heads, DK + DV, DK), BF16),
-            pltpu.VMEM((chips, heads, DK + DV, DK), BF16),
+            pltpu.VMEM((each, DK + DV, DK), BF16),
+            pltpu.VMEM((chips, each, DK + DV, DK), BF16),
             pltpu.VMEM((heads, DV, DK), F32),
-            pltpu.VMEM((groups, streams, local, heads // groups * DV), BF16),
+            pltpu.VMEM((DV, DK), F32),
+            pltpu.VMEM((heads, streams, local, DV), BF16),
             dma((streams,)),
             dma((1,)),
             dma((1,)),
@@ -658,13 +688,15 @@
             dma((senders, streams)),
             dma((1,)),
             dma((1,)),
-            dma((groups,)),
-            dma((groups,)),
-            dma((chips, groups)),
-            dma((chips, groups)),
-            dma((streams, groups)),
-            dma((streams, groups)),
-            dma((groups,)),
+            dma((2,)),
+            dma((2,)),
+            dma((chips, each)),
+            dma((chips, each)),
+            dma((each,)),
+            dma((each,)),
+            dma((1,)),
+            dma((streams,)),
+            dma((1,)),
         ],
         compiler_params=pltpu.CompilerParams(collective_id=0, has_side_effects=True),
     )(

time: 87.8 us -> 84.3 us (0.960)
  Pallas kernels: 85.8 us -> 82.3 us
    pallas_call x1, Pallas kernels: 85.8 us -> 82.3 us  [shards(): pl.pallas_call(functools.partial(layer_kernel, streams, places, heads, se...]
where the time goes in v3:
time: 84.3 us; the launch traced here: 84.2 us
  Pallas kernels  82.3 us (98%)
  local copies, waits for them, and re-layouts  1.88 us (2%)
    pallas_call x1, Pallas kernels, shards(): pl.pallas_call(functools.partial(layer_kernel, streams, places, heads, se...  82.3 us
    unnamed x1, local copies, waits for them, and re-layouts  1.88 us

profile of v3, /device:TPU:4, one launch (start us, length us, event | category | flops | bytes accessed | tf_op | source)
XLA Modules:
  0.0 84.2 jit_solution(16809259151873133911)
XLA Ops:
  0.0 82.3 %shard_map.91 = bf16[128,2048]{1,0:T(8,128)(2,1)} custom-call(bf16[128,2048]{1,0:T(8,128)(2,1)} %tok_ref.1, bf16[512,2048]{1,0:T(8,128)(2,1)} %wq_ref.1, bf16[512,2048]{1,0:T(8,128)(2,1)} %wk_ref.1, bf16[512,2048]{1,0:T(8,128)(2,1)} %wv_ref.1, bf16[16,512]{1,0:T(8,128)(2,1)} %bitcast.5, bf16[16,512]{1,0:T(8,128)(2,1)} %bitcast.6, f32[1,16]{1,0:T(1,128)} %bitcast.7, ...), custom_call_target="tpu_custom_call" | custom-call | tf_op jit(solution)/shard_map/pallas_call | solution.py:652
  82.3 1.9 %copy.11 = bf16[128,2048]{1,0:T(8,128)(2,1)} copy(bf16[128,2048]{1,0:T(8,128)(2,1)} %shard_map.91) | data formatting | bytes 1048576

commit v4 on v3

--- a/solution.py
+++ b/solution.py
@@ -12,6 +12,7 @@
 DV = 128
 CHUNK = 128
 PIECES = 4
+DIRECT = 0
 F32 = jnp.float32
 BF16 = jnp.bfloat16
 
@@ -71,6 +72,10 @@
     stage,
     gates,
     cum_row,
+    k_ref,
+    decays_ref,
+    growth_ref,
+    wu_ref,
     step_ref,
     run_ref,
     read_ref,
@@ -92,6 +97,7 @@
     gate_sib,
     right_sem,
     left_sem,
+    across_send,
     tok_recv,
     cross_send,
     cross_recv,
@@ -181,7 +187,12 @@
             own_sem.at[0],
         ).start()
 
-    others = [lax.rem(chip + i, chips) * 2 + core for i in range(1, chips)]
+    square = chips == 4 and paired and share % 32 == 0
+    if square:
+        beyond = [chip + 1 - 2 * (chip % 2), lax.rem(chip + 2, chips), 3 - chip]
+    else:
+        beyond = [lax.rem(chip + i, chips) for i in range(1, chips)]
+    others = [c * 2 + core for c in beyond]
     peers = [(t, lax.rem(z + i, streams)) for i in near]
     peers += [(sibling, z)] + [(o, z) for o in others]
     barrier = pltpu.get_barrier_semaphore()
@@ -243,6 +254,18 @@
         here = full.at[s, rows_of(k)]
         return remote(here, here, plane_send.at[0], plane_recv.at[k, s], (others[0], z))
 
+    direct = range(PIECES - DIRECT, PIECES) if streams > 2 else range(0)
+
+    def relayed(k, p):
+        return not (k == streams - 2 and p in direct)
+
+    def across(p):
+        at = pl.ds(p * part, part)
+        dest = jnp.where(z == 0, streams - 1, 0)
+        return remote(
+            tok_ref.at[at], x_ref.at[z, at], across_send.at[0], tok_recv.at[z, p], (t, dest)
+        )
+
     def token_step(k, pieces):
         for p in pieces:
 
@@ -250,17 +273,21 @@
             def _():
                 line(z - k, p, True, False).wait_recv()
 
-                @pl.when(z < streams - 1)
-                def _():
-                    line(z - k, p, True, False).start()
+                if relayed(k, p):
+
+                    @pl.when(z < streams - 1)
+                    def _():
+                        line(z - k, p, True, False).start()
 
             @pl.when(z + k < streams)
             def _():
                 line(z + k, p, False, False).wait_recv()
 
-                @pl.when(z > 0)
-                def _():
-                    line(z + k, p, False, False).start()
+                if relayed(k, p):
+
+                    @pl.when(z > 0)
+                    def _():
+                        line(z + k, p, False, False).start()
 
     def send_shares():
         for i in near:
@@ -281,39 +308,73 @@
         def _():
             line(z, p, False, True).start()
 
-    def spread():
-        for i in near:
-            s = lax.rem(z + i, streams)
-            crossed(i).wait_recv()
-            for j in range(1, chips):
-                plane(j, s).start()
-            beside(mine, s).start()
-
-    only(is_sender, spread)
-    for i in near:
-        gate_in(i).wait_recv()
-        gate_on(i).start()
-
-    def pass_on(i):
+    @pl.when((z == 0) | (z == streams - 1))
+    def _():
+        for p in direct:
+            across(p).start()
+
+    def forward(i, s):
+        at = pl.multiple_of((beyond[i - 1] * 2 + core) * share + (i - 1) * (share // 2), 16)
+        here = full.at[s, pl.ds(at, share // 2)]
+        k = beyond[i - 1] * 2 + core
+        return remote(
+            here, here, plane_send.at[3], plane_recv.at[k, s], (others[2 - i], z)
+        )
+
+    def spread(n):
+        s = lax.rem(z + n, streams)
+        crossed(n).wait_recv()
+        for j in range(1, 3 if square else chips):
+            plane(j, s).start()
+        beside(mine, s).start()
+
+    def pass_on(i, n):
         if i == 0:
             if paired:
                 return
             cond = active & (chip != base)
         else:
             cond = active
-        k = slot(i)
+        k = beyond[i - 1] * 2 + core if square else slot(i)
 
         def body():
-            for n in near:
-                s = lax.rem(z + n, streams)
-                landed(k, s).wait_recv()
-                beside(k, s).start()
+            s = lax.rem(z + n, streams)
+            landed(k, s).wait_recv()
+            if square and i < 3:
+                forward(i, s).start()
+            beside(k, s).start()
 
         only(cond, body)
 
-    token_step(1, range(PIECES))
-    for i in range(origins):
-        pass_on(i)
+    def share_gates():
+        for i in near:
+            gate_in(i).wait_recv()
+            gate_on(i).start()
+
+    if square:
+        for at, n in enumerate(near):
+            spread(n)
+            if at > 0:
+                pass_on(1, near[at - 1])
+                pass_on(2, near[at - 1])
+        share_gates()
+        for n in near[:-2]:
+            pass_on(3, n)
+        token_step(1, [0])
+        pass_on(1, near[-1])
+        pass_on(2, near[-1])
+        for p, n in enumerate(near[-2:]):
+            pass_on(3, n)
+            token_step(1, [p + 1])
+        token_step(1, range(1 + len(near[-2:]), PIECES))
+    else:
+        for n in near:
+            only(is_sender, functools.partial(spread, n))
+        share_gates()
+        token_step(1, range(PIECES))
+        for n in near:
+            for i in range(origins):
+                pass_on(i, n)
     own_tok.wait()
     drain(full.at[z], own_sem.at[0])
     drain(gates.at[0, pl.ds(0, streams - 1)], gate_sib.at[0])
@@ -348,6 +409,21 @@
 
     def split(a):
         return jnp.stack([a[:, h * DK : (h + 1) * DK] for h in range(heads)])
+
+    def project(x, j):
+        w = full[:, :, j * span : (j + 1) * span].reshape(streams * depth, span)
+        return split(contract(x, w, (((1,), (0,)), ((), ()))))
+
+    def reads(n):
+        at, _ = turn(n)
+        raw_q = project(x_ref[at], 0)
+        q = (
+            raw_q * lax.rsqrt(jnp.sum(raw_q * raw_q, -1, keepdims=True) + 1e-06) * DK ** (-0.5)
+        ).astype(BF16)
+        scores = contract(q, k_ref[...], (((2,), (2,)), ((0,), (0,))))
+        mwu = dot3(decays_ref[...] * scores, wu_ref[...], 2, 1, 1)
+        query_ref[:, at] = growth_ref[...] * q.astype(F32) - mwu[:, :, :DK]
+        read_ref[:, at] = mwu[:, :, DK:]
 
     def process(n):
         at, leftward = turn(n)
@@ -367,26 +443,20 @@
         b = columns(beta, 0)
         g_row = jnp.stack([cum_row[pl.ds(z * heads + h, 1), :] for h in range(heads)])
 
-        def project(j):
-            w = full[:, :, j * span : (j + 1) * span].reshape(streams * depth, span)
-            return split(contract(x, w, (((1,), (0,)), ((), ()))))
-
-        raw_k = project(1)
+        raw_k = project(x, 1)
         k = (raw_k * lax.rsqrt(jnp.sum(raw_k * raw_k, -1, keepdims=True) + 1e-06)).astype(BF16)
-        raw_q = project(0)
-        q = (
-            raw_q * lax.rsqrt(jnp.sum(raw_q * raw_q, -1, keepdims=True) + 1e-06) * DK ** (-0.5)
-        ).astype(BF16)
-        v = project(2).astype(BF16).astype(F32)
+        v = project(x, 2).astype(BF16).astype(F32)
         g_last = g[:, CHUNK - 1 :, :]
         growth = jnp.exp(g)
         tail = jnp.exp(g_last - g)
         whole = jnp.exp(g_last)
 
-        pair = contract(jnp.concatenate([k, q], 1), k, (((2,), (2,)), ((0,), (0,))))
-        spread_ = jnp.exp(jnp.where(low[None], g - g_row, 0.0))
-        lmat = jnp.where(strict[None], b * spread_ * pair[:, :CHUNK], 0.0)
-        mmat = jnp.where(low[None], spread_ * pair[:, CHUNK:], 0.0)
+        pair = contract(k, k, (((2,), (2,)), ((0,), (0,))))
+        decays = jnp.exp(jnp.where(low[None], g - g_row, 0.0))
+        lmat = jnp.where(strict[None], b * decays * pair, 0.0)
+        k_ref[...] = k
+        decays_ref[...] = jnp.where(low[None], decays, 0.0)
+        growth_ref[...] = jnp.broadcast_to(growth, (heads, CHUNK, DK))
 
         inverse = None
         size = 1
@@ -404,6 +474,7 @@
         kf = k.astype(F32)
         right = jnp.concatenate([(b * growth) * kf, b * v], 2)
         wu = dot3(inverse, right, 2, 1, 1)
+        wu_ref[...] = wu
         jumps = dot3(jnp.swapaxes(wu, 1, 2), tail * kf, 2, 1, 1)
         step_map = jnp.concatenate([whole * eye[None] - jumps[:, :DK], jumps[:, DK:]], 1)
         step_ref[at] = step_map
@@ -421,9 +492,6 @@
             give(0).start()
             give_rest(lambda copy: copy.start())
             run_ref[...] = run
-        mwu = dot3(mmat, wu, 2, 1, 1)
-        query_ref[:, at] = growth * q.astype(F32) - mwu[:, :, :DK]
-        read_ref[:, at] = mwu[:, :, DK:]
 
     def join_maps(before, after):
         both = dot3(before, after[:, :DK], 2, 1, 1)
@@ -466,7 +534,11 @@
     for n in range(streams):
         process(n)
         if n == 0 and streams > 2:
-            token_step(2, range(PIECES // 2))
+            token_step(2, [0])
+        if n < streams - 1:
+            reads(n)
+        if n == 0 and streams > 2:
+            token_step(2, range(1, PIECES // 2))
         elif n == 1 and streams > 2:
             token_step(2, range(PIECES // 2, PIECES))
         elif 2 <= n < streams - 1:
@@ -570,8 +642,9 @@
             outgoing(h, i).start()
         own_out(h).start()
 
+    join()
+    reads(streams - 1)
     carries()
-    join()
     prefixes()
     for n in range(each):
         enter(n)
@@ -622,15 +695,25 @@
 
     drain(gates.at[0, pl.ds(0, streams - 1)], gate_send.at[0])
     drain(gates.at[0, pl.ds(0, streams - 1)], gate_pass.at[0])
+
+    def whole_of(k):
+        return local - part * len(direct) if k == streams - 2 else local
+
+    if len(direct) > 0:
+
+        @pl.when((z == 0) | (z == streams - 1))
+        def _():
+            drain(x_ref.at[z, pl.ds(0, part * len(direct))], across_send.at[0])
+
     for k in range(streams):
 
         @pl.when((z >= k) & (z < streams - 1))
         def _():
-            drain(x_ref.at[z - k], right_sem.at[z - k])
+            drain(x_ref.at[z - k, pl.ds(0, whole_of(k))], right_sem.at[z - k])
 
         @pl.when((z + k < streams) & (z > 0))
         def _():
-            drain(x_ref.at[z + k], left_sem.at[z + k])
+            drain(x_ref.at[z + k, pl.ds(0, whole_of(k))], left_sem.at[z + k])
 
 
 def shards(
@@ -660,6 +743,10 @@
             pltpu.VMEM((streams, share, width), BF16),
             pltpu.VMEM((2, streams, HEADS, depth), BF16),
             pltpu.VMEM((HEADS, CHUNK), F32),
+            pltpu.VMEM((heads, CHUNK, DK), BF16),
+            pltpu.VMEM((heads, CHUNK, CHUNK), F32),
+            pltpu.VMEM((heads, CHUNK, DK), F32),
+            pltpu.VMEM((heads, CHUNK, DK + DV), F32),
             pltpu.VMEM((streams, heads, DK + DV, DK), F32),
             pltpu.VMEM((heads, DK + DV, DK), F32),
             pltpu.VMEM((heads, streams, CHUNK, DV), F32),
@@ -681,6 +768,7 @@
             dma((1,)),
             dma((streams,)),
             dma((streams,)),
+            dma((1,)),
             dma((streams, PIECES)),
             dma((1,)),
             dma((streams,)),

time: 84.3 us -> 79.5 us (0.943)
  Pallas kernels: 82.3 us -> 77.1 us
    pallas_call x1, Pallas kernels: 82.3 us -> 77.1 us  [shards(): pl.pallas_call(functools.partial(layer_kernel, streams, places, heads, se...]
where the time goes in v4:
time: 79.5 us; the launch traced here: 78.9 us
  Pallas kernels  77.1 us (97%)
  local copies, waits for them, and re-layouts  1.88 us (2%)
    pallas_call x1, Pallas kernels, shards(): pl.pallas_call(functools.partial(layer_kernel, streams, places, heads, se...  77.1 us
    unnamed x1, local copies, waits for them, and re-layouts  1.88 us

profile of v4, /device:TPU:4, one launch (start us, length us, event | category | flops | bytes accessed | tf_op | source)
XLA Modules:
  0.0 78.9 jit_solution(16869141465673954163)
XLA Ops:
  0.0 77.1 %shard_map.91 = bf16[128,2048]{1,0:T(8,128)(2,1)} custom-call(bf16[128,2048]{1,0:T(8,128)(2,1)} %tok_ref.1, bf16[512,2048]{1,0:T(8,128)(2,1)} %wq_ref.1, bf16[512,2048]{1,0:T(8,128)(2,1)} %wk_ref.1, bf16[512,2048]{1,0:T(8,128)(2,1)} %wv_ref.1, bf16[16,512]{1,0:T(8,128)(2,1)} %bitcast.5, bf16[16,512]{1,0:T(8,128)(2,1)} %bitcast.6, f32[1,16]{1,0:T(1,128)} %bitcast.7, ...), custom_call_target="tpu_custom_call" | custom-call | tf_op jit(solution)/shard_map/pallas_call | solution.py:735
  77.1 1.9 %copy.11 = bf16[128,2048]{1,0:T(8,128)(2,1)} copy(bf16[128,2048]{1,0:T(8,128)(2,1)} %shard_map.91) | data formatting | bytes 1048576

commit v5 on v4

--- a/solution.py
+++ b/solution.py
@@ -41,10 +41,10 @@
     return both[..., :half] + both[..., half:]
 
 
-def dot2(a, b, ca, cb):
-    ah, al = halves(a)
+def dot2(a, b):
+    bh, bl = halves(b)
     return contract(
-        jnp.concatenate([ah, al], ca), jnp.concatenate([b, b], cb), (((ca,), (cb,)), ((), ()))
+        jnp.concatenate([a, a], 1), jnp.concatenate([bh, bl], 0), (((1,), (0,)), ((), ()))
     )
 
 
@@ -313,6 +313,9 @@
         for p in direct:
             across(p).start()
 
+    def quarter(i):
+        return range(i * (PIECES // 4), (i + 1) * (PIECES // 4))
+
     def forward(i, s):
         at = pl.multiple_of((beyond[i - 1] * 2 + core) * share + (i - 1) * (share // 2), 16)
         here = full.at[s, pl.ds(at, share // 2)]
@@ -360,13 +363,13 @@
         share_gates()
         for n in near[:-2]:
             pass_on(3, n)
-        token_step(1, [0])
+        token_step(1, quarter(0))
         pass_on(1, near[-1])
         pass_on(2, near[-1])
         for p, n in enumerate(near[-2:]):
             pass_on(3, n)
-            token_step(1, [p + 1])
-        token_step(1, range(1 + len(near[-2:]), PIECES))
+            token_step(1, quarter(p + 1))
+        token_step(1, range((1 + len(near[-2:])) * (PIECES // 4), PIECES))
     else:
         for n in near:
             only(is_sender, functools.partial(spread, n))
@@ -448,7 +451,7 @@
         v = project(x, 2).astype(BF16).astype(F32)
         g_last = g[:, CHUNK - 1 :, :]
         growth = jnp.exp(g)
-        tail = jnp.exp(g_last - g)
+        tail = jnp.exp(g_last - g_row)
         whole = jnp.exp(g_last)
 
         pair = contract(k, k, (((2,), (2,)), ((0,), (0,))))
@@ -475,8 +478,8 @@
         right = jnp.concatenate([(b * growth) * kf, b * v], 2)
         wu = dot3(inverse, right, 2, 1, 1)
         wu_ref[...] = wu
-        jumps = dot3(jnp.swapaxes(wu, 1, 2), tail * kf, 2, 1, 1)
-        step_map = jnp.concatenate([whole * eye[None] - jumps[:, :DK], jumps[:, DK:]], 1)
+        jumps = dot3(tail * jnp.swapaxes(kf, 1, 2), wu, 2, 1, 1)
+        step_map = jnp.concatenate([whole * eye[None] - jumps[:, :, :DK], jumps[:, :, DK:]], 2)
         step_ref[at] = step_map
         if n == 0:
             run = step_map
@@ -494,8 +497,8 @@
             run_ref[...] = run
 
     def join_maps(before, after):
-        both = dot3(before, after[:, :DK], 2, 1, 1)
-        return jnp.concatenate([both[:, :DK], both[:, DK:] + after[:, DK:]], 1)
+        both = dot3(after[:, :, :DK], before, 2, 1, 1)
+        return jnp.concatenate([both[:, :, :DK], both[:, :, DK:] + after[:, :, DK:]], 2)
 
     mine_at = core * each if halved else 0
     theirs_at = (1 - core) * each if halved else 0
@@ -522,7 +525,7 @@
     def to_chip(n, source, dest):
         src, dst = total.at[n], got.at[source, n]
         if source == 0:
-            src, dst = total.at[n, pl.ds(DK, DV)], got.at[0, n, pl.ds(DK, DV)]
+            src, dst = total.at[n, :, pl.ds(DK, DV)], got.at[0, n, :, pl.ds(DK, DV)]
         return remote(
             src, dst, chip_send.at[dest, n], chip_recv.at[source, n], (dest * 2 + core, z)
         )
@@ -533,14 +536,12 @@
 
     for n in range(streams):
         process(n)
-        if n == 0 and streams > 2:
-            token_step(2, [0])
+        if n < 2 < streams:
+            token_step(2, quarter(2 * n))
         if n < streams - 1:
             reads(n)
-        if n == 0 and streams > 2:
-            token_step(2, range(1, PIECES // 2))
-        elif n == 1 and streams > 2:
-            token_step(2, range(PIECES // 2, PIECES))
+        if n < 2 < streams:
+            token_step(2, quarter(2 * n + 1))
         elif 2 <= n < streams - 1:
             token_step(n + 1, range(PIECES))
 
@@ -570,7 +571,7 @@
 
     def prefixes():
         for c in range(1, streams):
-            both = dot3(query_ref[:, c], step_ref[c - 1], 2, 2, 1)
+            both = dot3(query_ref[:, c], step_ref[c - 1], 2, 1, 1)
             query_ref[:, c] = both[:, :, :DK]
             read_ref[:, c] = read_ref[:, c] + both[:, :, DK:]
 
@@ -579,7 +580,7 @@
 
         @pl.when(chip == 0)
         def _():
-            prev[h] = jnp.zeros((DV, DK), F32)
+            prev[h] = jnp.zeros((DK, DV), F32)
 
         for source in range(chips - 1):
 
@@ -587,10 +588,10 @@
             def _():
                 to_chip(n, source, chip).wait_recv()
                 if source == 0:
-                    prev[h] = got[0, n, DK:].astype(F32)
+                    prev[h] = got[0, n, :, DK:].astype(F32)
                 else:
-                    prev[h] = dot2(prev[h], got[source, n, :DK], 1, 0) + got[
-                        source, n, DK:
+                    prev[h] = dot2(got[source, n, :, :DK], prev[h]) + got[
+                        source, n, :, DK:
                     ].astype(F32)
 
         if halved:
@@ -604,7 +605,7 @@
 
         @pl.when(chip == 0)
         def _():
-            prev[h] = jnp.zeros((DV, DK), F32)
+            prev[h] = jnp.zeros((DK, DV), F32)
 
         @pl.when(chip > 0)
         def _():
@@ -631,9 +632,9 @@
 
         @pl.when(core == 1)
         def _():
-            state[...] = dot2(carried, sib_map[h, :DK], 1, 0) + sib_map[h, DK:].astype(F32)
-
-        reads = dot3(query_ref[h].reshape(streams * local, DK), state[...], 1, 1)
+            state[...] = dot2(sib_map[h, :, :DK], carried) + sib_map[h, :, DK:].astype(F32)
+
+        reads = dot3(query_ref[h].reshape(streams * local, DK), state[...], 1, 0)
         read = read_ref[h].reshape(streams * local, DV) + reads
         readout = read.astype(BF16).astype(F32)
         scale = lax.rsqrt(jnp.mean(readout * readout, -1, keepdims=True) + 1e-06)
@@ -734,9 +735,9 @@
     dma = pltpu.SemaphoreType.DMA
     return pl.pallas_call(
         functools.partial(layer_kernel, streams, places, heads, senders),
-        out_shape=jax.ShapeDtypeStruct((local, HEADS * DV), BF16),
+        out_shape=pltpu.VMEM((local, HEADS * DV), BF16),
         in_specs=[any_space] * 6 + [vmem] * 3,
-        out_specs=any_space,
+        out_specs=vmem,
         scratch_shapes=[
             pltpu.VMEM((streams, local, features), BF16),
             pltpu.VMEM((streams, depth, width), BF16),
@@ -747,16 +748,16 @@
             pltpu.VMEM((heads, CHUNK, CHUNK), F32),
             pltpu.VMEM((heads, CHUNK, DK), F32),
             pltpu.VMEM((heads, CHUNK, DK + DV), F32),
-            pltpu.VMEM((streams, heads, DK + DV, DK), F32),
-            pltpu.VMEM((heads, DK + DV, DK), F32),
+            pltpu.VMEM((streams, heads, DK, DK + DV), F32),
+            pltpu.VMEM((heads, DK, DK + DV), F32),
             pltpu.VMEM((heads, streams, CHUNK, DV), F32),
             pltpu.VMEM((heads, streams, CHUNK, DK), F32),
-            pltpu.VMEM((heads, DK + DV, DK), BF16),
-            pltpu.VMEM((heads, DK + DV, DK), BF16),
-            pltpu.VMEM((each, DK + DV, DK), BF16),
-            pltpu.VMEM((chips, each, DK + DV, DK), BF16),
-            pltpu.VMEM((heads, DV, DK), F32),
-            pltpu.VMEM((DV, DK), F32),
+            pltpu.VMEM((heads, DK, DK + DV), BF16),
+            pltpu.VMEM((heads, DK, DK + DV), BF16),
+            pltpu.VMEM((each, DK, DK + DV), BF16),
+            pltpu.VMEM((chips, each, DK, DK + DV), BF16),
+            pltpu.VMEM((heads, DK, DV), F32),
+            pltpu.VMEM((DK, DV), F32),
             pltpu.VMEM((heads, streams, local, DV), BF16),
             dma((streams,)),
             dma((1,)),

time: 79.5 us -> 78.2 us (0.984)
  local copies, waits for them, and re-layouts: 1.88 us -> 0.8 us
    unnamed x1, local copies, waits for them, and re-layouts: 1.88 us -> 0.8 us
where the time goes in v5:
time: 78.2 us; the launch traced here: 78.1 us
  Pallas kernels  77.3 us (99%)
  local copies, waits for them, and re-layouts  0.8 us (1%)
    pallas_call x1, Pallas kernels, shards(): pl.pallas_call(functools.partial(layer_kernel, streams, places, heads, se...  77.3 us

profile of v5, /device:TPU:4, one launch (start us, length us, event | category | flops | bytes accessed | tf_op | source)
XLA Modules:
  0.0 78.1 jit_solution(11267546995145771032)
XLA Ops:
  0.0 77.3 %shard_map.91 = bf16[128,2048]{1,0:T(8,128)(2,1)S(1)} custom-call(bf16[128,2048]{1,0:T(8,128)(2,1)} %tok_ref.1, bf16[512,2048]{1,0:T(8,128)(2,1)} %wq_ref.1, bf16[512,2048]{1,0:T(8,128)(2,1)} %wk_ref.1, bf16[512,2048]{1,0:T(8,128)(2,1)} %wv_ref.1, bf16[16,512]{1,0:T(8,128)(2,1)} %bitcast.5, bf16[16,512]{1,0:T(8,128)(2,1)} %bitcast.6, f32[1,16]{1,0:T(1,128)} %bitcast.7, ...), custom_call_target="tpu_custom_call" | custom-call | tf_op jit(solution)/shard_map/pallas_call | solution.py:736
  77.3 0.8 %copy.11 = bf16[128,2048]{1,0:T(8,128)(2,1)} copy(bf16[128,2048]{1,0:T(8,128)(2,1)S(1)} %shard_map.91) | data formatting | bytes 1048576

commit v6 on v5

--- a/solution.py
+++ b/solution.py
@@ -131,6 +131,7 @@
     local, features = tok_ref.shape
     part = local // PIECES
     near = around(streams)
+    ranks = range(1, streams)
     span = heads * DK
     halved = heads % 2 == 0
     each = heads // 2 if halved else heads
@@ -161,6 +162,18 @@
     def slot(i):
         at = lax.rem(base + i * step, chips)
         return 2 * at + core if paired else at // step
+
+    def turn(n):
+        fewer = jnp.minimum(z, streams - 1 - z)
+        left = z * 2 >= streams
+        both = n <= 2 * fewer
+        k = jnp.where(both, (n + 1) // 2, n - fewer)
+        leftward = jnp.where(both, jnp.where(left, n % 2 == 0, n % 2 == 1), left)
+        at = jnp.where(leftward, z - k, z + k)
+        return (z, None) if n == 0 else (at, leftward)
+
+    def partner(n):
+        return turn(n)[0]
 
     weights = (wq_ref, wk_ref, wv_ref)
     my_rows = pl.ds(pl.multiple_of(mine * share, share), share)
@@ -240,10 +253,13 @@
             stage.at[s], full.at[s, rows_of(mine)], cross_send.at[0], cross_recv.at[s], (t, s)
         )
 
+    def origin(k):
+        return k // 2 if paired else k
+
     def plane(i, s):
         here = full.at[s, rows_of(mine)]
         return remote(
-            here, here, plane_send.at[i], plane_recv.at[mine, s], (others[i - 1], z)
+            here, here, plane_send.at[i], plane_recv.at[origin(mine), s], (others[i - 1], z)
         )
 
     def beside(k, s):
@@ -252,7 +268,7 @@
 
     def landed(k, s):
         here = full.at[s, rows_of(k)]
-        return remote(here, here, plane_send.at[0], plane_recv.at[k, s], (others[0], z))
+        return remote(here, here, plane_send.at[0], plane_recv.at[origin(k), s], (others[0], z))
 
     direct = range(PIECES - DIRECT, PIECES) if streams > 2 else range(0)
 
@@ -321,7 +337,7 @@
         here = full.at[s, pl.ds(at, share // 2)]
         k = beyond[i - 1] * 2 + core
         return remote(
-            here, here, plane_send.at[3], plane_recv.at[k, s], (others[2 - i], z)
+            here, here, plane_send.at[3], plane_recv.at[origin(k), s], (others[2 - i], z)
         )
 
     def spread(n):
@@ -394,15 +410,6 @@
     lower_ones = jnp.where(low, 1.0, 0.0).astype(BF16)
     lane = lax.broadcasted_iota(jnp.int32, (CHUNK, HEADS), 1)
 
-    def turn(n):
-        fewer = jnp.minimum(z, streams - 1 - z)
-        left = z * 2 >= streams
-        both = n <= 2 * fewer
-        k = jnp.where(both, (n + 1) // 2, n - fewer)
-        leftward = jnp.where(both, jnp.where(left, n % 2 == 0, n % 2 == 1), left)
-        at = jnp.where(leftward, z - k, z + k)
-        return (z, None) if n == 0 else (at, leftward)
-
     def columns(a, first):
         picked = [
             jnp.sum(jnp.where(lane == z * heads + h, a, 0.0), -1, keepdims=True)
@@ -615,8 +622,8 @@
         at = pl.multiple_of((source * heads + h) * DV, DV)
         return out_ref.at[:, pl.ds(at, DV)]
 
-    def outgoing(h, i):
-        dest = lax.rem(z + i, streams)
+    def outgoing(h, n):
+        dest = partner(n)
         return remote(
             mixed.at[h, dest], spot(h, z), out_send.at[0], out_recv.at[z], (t, dest)
         )
@@ -639,8 +646,8 @@
         readout = read.astype(BF16).astype(F32)
         scale = lax.rsqrt(jnp.mean(readout * readout, -1, keepdims=True) + 1e-06)
         mixed[h] = (readout * scale * gain_ref[...]).astype(BF16).reshape(streams, local, DV)
-        for i in far:
-            outgoing(h, i).start()
+        for n in reversed(ranks):
+            outgoing(h, n).start()
         own_out(h).start()
 
     join()
@@ -774,7 +781,7 @@
             dma((1,)),
             dma((streams,)),
             dma((chips,)),
-            dma((senders, streams)),
+            dma((senders // 2 if senders == places else senders, streams)),
             dma((1,)),
             dma((1,)),
             dma((2,)),

time: 78.2 us -> 78.1 us (level)
  no operation moved by 1% of the time
where the time goes in v6:
time: 78.1 us; the launch traced here: 77.9 us
  Pallas kernels  77.1 us (99%)
  local copies, waits for them, and re-layouts  0.8 us (1%)
    pallas_call x1, Pallas kernels, shards(): pl.pallas_call(functools.partial(layer_kernel, streams, places, heads, se...  77.1 us

profile of v6, /device:TPU:4, one launch (start us, length us, event | category | flops | bytes accessed | tf_op | source)
XLA Modules:
  0.0 77.9 jit_solution(275434872646739780)
XLA Ops:
  0.0 77.1 %shard_map.91 = bf16[128,2048]{1,0:T(8,128)(2,1)S(1)} custom-call(bf16[128,2048]{1,0:T(8,128)(2,1)} %tok_ref.1, bf16[512,2048]{1,0:T(8,128)(2,1)} %wq_ref.1, bf16[512,2048]{1,0:T(8,128)(2,1)} %wk_ref.1, bf16[512,2048]{1,0:T(8,128)(2,1)} %wv_ref.1, bf16[16,512]{1,0:T(8,128)(2,1)} %bitcast.5, bf16[16,512]{1,0:T(8,128)(2,1)} %bitcast.6, f32[1,16]{1,0:T(1,128)} %bitcast.7, ...), custom_call_target="tpu_custom_call" | custom-call | tf_op jit(solution)/shard_map/pallas_call | solution.py:743
  77.2 0.8 %copy.11 = bf16[128,2048]{1,0:T(8,128)(2,1)} copy(bf16[128,2048]{1,0:T(8,128)(2,1)S(1)} %shard_map.91) | data formatting | bytes 1048576
